TPU v7x, 512 devices: a whole 4x8x8 slice. The times are simulated.
512 devices in a mesh: seq: 64 (over x, y, core), tp: 8 (over z).
Axes of the slice: x: 4, y: 8, z: 8, core: 2. Of those that a mesh axis runs over, the one named last changes fastest.
Arguments:
- queries: bfloat16 [16384, 4096], P('seq', 'tp'), may hold values from -50 to 50
- keys: bfloat16 [16384, 4096], P('seq', 'tp'), may hold values from -4 to 4
- values: bfloat16 [16384, 4096], P('seq', 'tp'), may hold values from -18 to 18
- doc_lengths: int32 [32], replicated, may hold values from 1 to 2048, 16384 in all
- out_weight: bfloat16 [4096, 4096], P('tp', 'seq'), may hold values from -0.25 to 0.25
Outputs:
- projected: bfloat16 [16384, 4096], P('seq', 'tp')
Inputs may be any that keep to these rules, and one draw needn't show every extreme that they name: `doc_lengths`: document lengths in order, summing to 16384; the longest is exactly 2048.
All inputs are finite; a program needn't handle non-finite values.
Results may differ from a plain program's by a relative error of at most 0.015.
Values may be sent and summed in bfloat16 or wider, within the bound.
No kernel may reach another device: no remote copies, remote signals or barrier semaphores. Data moves between devices by JAX's collectives and lax.ppermute only.
A program may use at most 64 MiB of HBM per device.

v0:
```python
import math

import jax
import jax.numpy as jnp
from jax import lax
from jax.sharding import PartitionSpec as P

HD = 128
REACH = 8


def passed_along(value, axis, steps):
    count = lax.axis_size(axis)
    first, last = (max(0, -steps), min(count, count - steps))
    return lax.ppermute(value, axis, [(source, source + steps) for source in range(first, last)])


def doc_of(positions, doc_lengths):
    ends = jnp.cumsum(doc_lengths)
    return jnp.sum((ends[None, :] <= positions[:, None]).astype(jnp.int32), axis=1)


def absorb(carry, query_heads, query_ids, key_heads, value_heads, key_ids):
    run_max, run_sum, accum = carry
    scale = 1.0 / math.sqrt(HD)
    scores = (
        jnp.einsum("qhd,khd->hqk", query_heads, key_heads, preferred_element_type=jnp.float32)
        * scale
    )
    same = (query_ids[:, None] == key_ids[None, :])[None]
    scores = jnp.where(same, scores, -1e30)
    new_max = jnp.maximum(run_max, jnp.max(scores, axis=2))
    weights = jnp.where(same, jnp.exp(scores - new_max[:, :, None]), 0.0)
    factor = jnp.exp(run_max - new_max)
    run_sum = run_sum * factor + jnp.sum(weights, axis=2)
    accum = accum * factor[:, :, None] + jnp.einsum(
        "hqk,khd->hqd",
        weights.astype(jnp.bfloat16),
        value_heads,
        preferred_element_type=jnp.float32,
    )
    return (new_max, run_sum, accum)


def local(queries, keys, values, doc_lengths, out_weight):
    rows = queries.shape[0]
    heads_here = queries.shape[1] // HD
    seq_count = lax.axis_size("seq")
    total_rows = rows * seq_count
    index = lax.axis_index("seq")
    query_heads = queries.reshape(rows, heads_here, HD)
    query_ids = doc_of(index * rows + jnp.arange(rows, dtype=jnp.int32), doc_lengths)

    def absorb_block(carry, key_rows, value_rows, key_ids):
        key_heads = key_rows.reshape(key_rows.shape[0], heads_here, HD)
        value_heads = value_rows.reshape(value_rows.shape[0], heads_here, HD)
        return absorb(carry, query_heads, query_ids, key_heads, value_heads, key_ids)

    start_state = (
        jnp.full((heads_here, rows), -1e30, jnp.float32),
        jnp.zeros((heads_here, rows), jnp.float32),
        jnp.zeros((heads_here, rows, HD), jnp.float32),
    )
    below = []
    above = []
    moving = (keys, values)
    for distance in range(REACH):
        moving = passed_along((moving[0], moving[1]), "seq", 1)
        below.insert(0, moving)
    moving = (keys, values)
    for distance in range(REACH):
        moving = passed_along((moving[0], moving[1]), "seq", -1)
        above.append(moving)
    filler = jnp.zeros_like(keys)
    window_keys = jnp.concatenate(
        [pair[0] for pair in below] + [keys] + [pair[0] for pair in above] + [filler], axis=0
    )
    window_values = jnp.concatenate(
        [pair[1] for pair in below] + [values] + [pair[1] for pair in above] + [filler], axis=0
    )
    window_rows = (2 * REACH + 2) * rows
    offsets = jnp.arange(window_rows, dtype=jnp.int32)
    positions = (index - REACH) * rows + offsets
    inside = (positions >= 0) & (positions < total_rows) & (offsets < (2 * REACH + 1) * rows)
    window_ids = jnp.where(inside, doc_of(positions, doc_lengths), -1)
    span = 2 * rows

    def step_window(number, state):
        offset = number * span
        block_keys = lax.dynamic_slice_in_dim(window_keys, offset, span, 0)
        block_values = lax.dynamic_slice_in_dim(window_values, offset, span, 0)
        block_ids = lax.dynamic_slice_in_dim(window_ids, offset, span, 0)
        return absorb_block(state, block_keys, block_values, block_ids)

    final_state = lax.fori_loop(0, REACH + 1, step_window, start_state)
    run_max, run_sum, accum = final_state
    mixed = accum / run_sum[:, :, None]
    attended = jnp.transpose(mixed, (1, 0, 2)).reshape(rows, heads_here * HD).astype(jnp.bfloat16)
    partial_value = jnp.dot(
        attended,
        lax.all_gather(out_weight, "seq", axis=1, tiled=True),
        preferred_element_type=jnp.float32,
    )
    return lax.psum_scatter(
        partial_value.astype(jnp.bfloat16), "tp", scatter_dimension=1, tiled=True
    )


def solution(mesh):
    in_specs = (P("seq", "tp"), P("seq", "tp"), P("seq", "tp"), P(), P("tp", "seq"))
    out_specs = P("seq", "tp")
    return jax.shard_map(local, mesh=mesh, in_specs=in_specs, out_specs=out_specs, check_vma=False)
```

profile of v0, /device:TPU:16, one launch (start us, length us, event | category | flops | bytes accessed | tf_op | source)
XLA Modules:
  0.0 253.6 jit_solution(15434863907733873441)
XLA Ops:
  7.6 1.9 collective-permute-start.16
  9.6 3.6 %collective-permute-start.24 = (bf16[256,512]{0,1:T(8,128)(2,1)S(1)}, bf16[256,512]{0,1:T(8,128)(2,1)S(1)}, u32[]{:S(2)}, u32[]{:S(2)}) collective-permute-start(bf16[256,512]{0,1:T(8,128)(2,1)S(1)} %copy.29), channel_id=1, source_target_pairs={{8,0},{16,8},{24,16},{32,24},{40,32},{48,40},{56,48},{64,56},{72,6... | collective-permute-start | bytes 786440 | tf_op jit(solution)/shard_map/ppermute | solution.py:15
  14.3 1.9 collective-permute-start
  16.2 3.6 %collective-permute-start.8 = (bf16[256,512]{0,1:T(8,128)(2,1)S(1)}, bf16[256,512]{0,1:T(8,128)(2,1)S(1)}, u32[]{:S(2)}, u32[]{:S(2)}) collective-permute-start(bf16[256,512]{0,1:T(8,128)(2,1)S(1)} %copy.25), channel_id=1, source_target_pairs={{8,0},{16,8},{24,16},{32,24},{40,32},{48,40},{56,48},{64,56},{72,6... | collective-permute-start | bytes 786440 | tf_op jit(solution)/shard_map/ppermute | solution.py:15
  19.9 1.9 collective-permute-start.17
  21.8 3.6 %collective-permute-start.25 = (bf16[256,512]{0,1:T(8,128)(2,1)S(1)}, bf16[256,512]{0,1:T(8,128)(2,1)S(1)}, u32[]{:S(2)}, u32[]{:S(2)}) collective-permute-start(bf16[256,512]{0,1:T(8,128)(2,1)S(1)} %collective-permute-done.24), channel_id=1, source_target_pairs={{8,0},{16,8},{24,16},{32,24},{40,32},{48,40},{56,48},{64,56},{72,6... | collective-permute-start | bytes 786440 | tf_op jit(solution)/shard_map/ppermute | solution.py:15
  25.5 1.9 collective-permute-start.1
  27.4 3.6 %collective-permute-start.9 = (bf16[256,512]{0,1:T(8,128)(2,1)S(1)}, bf16[256,512]{0,1:T(8,128)(2,1)S(1)}, u32[]{:S(2)}, u32[]{:S(2)}) collective-permute-start(bf16[256,512]{0,1:T(8,128)(2,1)S(1)} %collective-permute-done.8), channel_id=1, source_target_pairs={{8,0},{16,8},{24,16},{32,24},{40,32},{48,40},{56,48},{64,56},{72,6... | collective-permute-start | bytes 786440 | tf_op jit(solution)/shard_map/ppermute | solution.py:15
  31.1 2.5 collective-permute-start.18
  33.6 3.1 %collective-permute-start.26 = (bf16[256,512]{0,1:T(8,128)(2,1)S(1)}, bf16[256,512]{0,1:T(8,128)(2,1)S(1)}, u32[]{:S(2)}, u32[]{:S(2)}) collective-permute-start(bf16[256,512]{0,1:T(8,128)(2,1)S(1)} %collective-permute-done.25), channel_id=1, source_target_pairs={{8,0},{16,8},{24,16},{32,24},{40,32},{48,40},{56,48},{64,56},{72,6... | collective-permute-start | bytes 786440 | tf_op jit(solution)/shard_map/ppermute | solution.py:15
  36.7 3.7 %collective-permute-start.2 = (bf16[256,512]{0,1:T(8,128)(2,1)S(1)}, bf16[256,512]{0,1:T(8,128)(2,1)S(1)}, u32[]{:S(2)}, u32[]{:S(2)}) collective-permute-start(bf16[256,512]{0,1:T(8,128)(2,1)S(1)} %collective-permute-done.1), channel_id=1, source_target_pairs={{0,8},{8,16},{16,24},{24,32},{32,40},{40,48},{48,56},{56,64},{64,7... | collective-permute-start | bytes 786440 | tf_op jit(solution)/shard_map/ppermute | solution.py:15
  40.4 1.9 collective-permute-start.10
  42.4 4.9 %collective-permute-start.19 = (bf16[256,512]{0,1:T(8,128)(2,1)S(1)}, bf16[256,512]{0,1:T(8,128)(2,1)S(1)}, u32[]{:S(2)}, u32[]{:S(2)}) collective-permute-start(bf16[256,512]{0,1:T(8,128)(2,1)S(1)} %collective-permute-done.18), channel_id=1, source_target_pairs={{0,8},{8,16},{16,24},{24,32},{32,40},{40,48},{48,56},{56,64},{64,7... | collective-permute-start | bytes 786440 | tf_op jit(solution)/shard_map/ppermute | solution.py:15
  47.3 1.9 collective-permute-start.27
  49.2 4.9 %collective-permute-start.3 = (bf16[256,512]{0,1:T(8,128)(2,1)S(1)}, bf16[256,512]{0,1:T(8,128)(2,1)S(1)}, u32[]{:S(2)}, u32[]{:S(2)}) collective-permute-start(bf16[256,512]{0,1:T(8,128)(2,1)S(1)} %collective-permute-done.2), channel_id=1, source_target_pairs={{0,8},{8,16},{16,24},{24,32},{32,40},{40,48},{48,56},{56,64},{64,7... | collective-permute-start | bytes 786440 | tf_op jit(solution)/shard_map/ppermute | solution.py:15
  54.1 1.9 collective-permute-start.11
  56.0 4.9 %collective-permute-start.20 = (bf16[256,512]{0,1:T(8,128)(2,1)S(1)}, bf16[256,512]{0,1:T(8,128)(2,1)}, u32[]{:S(2)}, u32[]{:S(2)}) collective-permute-start(bf16[256,512]{0,1:T(8,128)(2,1)S(1)} %collective-permute-done.19), channel_id=1, source_target_pairs={{0,8},{8,16},{16,24},{24,32},{32,40},{40,48},{48,56},{56,64},{64,7... | collective-permute-start | bytes 786440 | tf_op jit(solution)/shard_map/ppermute | solution.py:15
  60.9 1.9 collective-permute-start.28
  62.9 4.9 %collective-permute-start.4 = (bf16[256,512]{0,1:T(8,128)(2,1)S(1)}, bf16[256,512]{0,1:T(8,128)(2,1)}, u32[]{:S(2)}, u32[]{:S(2)}) collective-permute-start(bf16[256,512]{0,1:T(8,128)(2,1)S(1)} %collective-permute-done.3), channel_id=1, source_target_pairs={{0,8},{8,16},{16,24},{24,32},{32,40},{40,48},{48,56},{56,64},{64,7... | collective-permute-start | bytes 786440 | tf_op jit(solution)/shard_map/ppermute | solution.py:15
  67.7 1.9 collective-permute-start.12
  69.7 4.9 %collective-permute-start.21 = (bf16[256,512]{0,1:T(8,128)(2,1)}, bf16[256,512]{0,1:T(8,128)(2,1)}, u32[]{:S(2)}, u32[]{:S(2)}) collective-permute-start(bf16[256,512]{0,1:T(8,128)(2,1)} %collective-permute-done.20), channel_id=1, source_target_pairs={{0,8},{8,16},{16,24},{24,32},{32,40},{40,48},{48,56},{56,64},{64,7... | collective-permute-start | bytes 786440 | tf_op jit(solution)/shard_map/ppermute | solution.py:15
  74.7 1.9 collective-permute-start.29
  76.6 4.9 %collective-permute-start.5 = (bf16[256,512]{0,1:T(8,128)(2,1)}, bf16[256,512]{0,1:T(8,128)(2,1)}, u32[]{:S(2)}, u32[]{:S(2)}) collective-permute-start(bf16[256,512]{0,1:T(8,128)(2,1)} %collective-permute-done.4), channel_id=1, source_target_pairs={{0,8},{8,16},{16,24},{24,32},{32,40},{40,48},{48,56},{56,64},{64,7... | collective-permute-start | bytes 786440 | tf_op jit(solution)/shard_map/ppermute | solution.py:15
  81.5 1.9 collective-permute-start.13
  83.4 4.9 %collective-permute-start.22 = (bf16[256,512]{0,1:T(8,128)(2,1)}, bf16[256,512]{0,1:T(8,128)(2,1)}, u32[]{:S(2)}, u32[]{:S(2)}) collective-permute-start(bf16[256,512]{0,1:T(8,128)(2,1)} %collective-permute-done.21), channel_id=1, source_target_pairs={{0,8},{8,16},{16,24},{24,32},{32,40},{40,48},{48,56},{56,64},{64,7... | collective-permute-start | bytes 786440 | tf_op jit(solution)/shard_map/ppermute | solution.py:15
  90.0 1.9 collective-permute-start.30
  91.9 4.9 %collective-permute-start.6 = (bf16[256,512]{0,1:T(8,128)(2,1)}, bf16[256,512]{0,1:T(8,128)(2,1)}, u32[]{:S(2)}, u32[]{:S(2)}) collective-permute-start(bf16[256,512]{0,1:T(8,128)(2,1)} %collective-permute-done.5), channel_id=1, source_target_pairs={{0,8},{8,16},{16,24},{24,32},{32,40},{40,48},{48,56},{56,64},{64,7... | collective-permute-start | bytes 786440 | tf_op jit(solution)/shard_map/ppermute | solution.py:15
  96.8 1.9 collective-permute-start.14
  98.7 4.9 %collective-permute-start.23 = (bf16[256,512]{0,1:T(8,128)(2,1)}, bf16[256,512]{0,1:T(8,128)(2,1)}, u32[]{:S(2)}, u32[]{:S(2)}) collective-permute-start(bf16[256,512]{0,1:T(8,128)(2,1)} %collective-permute-done.22), channel_id=1, source_target_pairs={{0,8},{8,16},{16,24},{24,32},{32,40},{40,48},{48,56},{56,64},{64,7... | collective-permute-start | bytes 786440 | tf_op jit(solution)/shard_map/ppermute | solution.py:15
  105.0 1.4 fusion.13
  106.4 1.9 collective-permute-start.31
  108.4 4.9 %collective-permute-start.7 = (bf16[256,512]{0,1:T(8,128)(2,1)}, bf16[256,512]{0,1:T(8,128)(2,1)S(1)}, u32[]{:S(2)}, u32[]{:S(2)}) collective-permute-start(bf16[256,512]{0,1:T(8,128)(2,1)} %collective-permute-done.6), channel_id=1, source_target_pairs={{0,8},{8,16},{16,24},{24,32},{32,40},{40,48},{48,56},{56,64},{64,7... | collective-permute-start | bytes 786440 | tf_op jit(solution)/shard_map/ppermute | solution.py:15
  113.2 1.9 collective-permute-start.15
  126.3 1.2 constant_dynamic-update-slice_fusion.15
  127.5 1.2 constant_dynamic-update-slice_fusion.14
  132.0 2.2 copy-done.1
  134.2 40.1 %while.18 = (s32[]{:T(128)}, f32[4,256]{1,0:T(4,128)S(1)}, f32[4,256]{1,0:T(4,128)S(1)}, f32[4,256,128]{2,1,0:T(8,128)S(1)}, s32[256]{0:T(256)S(1)}, /*index=5*/...) while((s32[]{:T(128)}, f32[4,256]{1,0:T(4,128)S(1)}, ...), condition=%wide.region_6.7_spmd.clone, body=%wide.region_3.6_spmd.clone.sunk | while | flops 275780608 | bytes 11345087 | solution.py:95
  135.1 1.3 constant_dynamic-slice_fusion.3
  139.5 1.3 constant_dynamic-slice_fusion.3
  144.0 1.3 constant_dynamic-slice_fusion.3
  148.4 1.3 constant_dynamic-slice_fusion.3
  152.9 1.3 constant_dynamic-slice_fusion.3
  157.4 1.3 constant_dynamic-slice_fusion.3
  161.8 1.3 constant_dynamic-slice_fusion.3
  166.3 1.3 constant_dynamic-slice_fusion.3
  170.7 1.3 constant_dynamic-slice_fusion.3
  174.6 4.9 %convolution_convert_fusion = bf16[256,4096]{1,0:T(8,128)(2,1)} fusion(bf16[256,512]{0,1:T(8,128)(2,1)S(1)} %bitcast.41, bf16[512,4096]{0,1:T(8,128)(2,1)} %all-gather.2.cloned.1.call-done), kind=kOutput, calls=%fused_computation.21 | convolution fusion | flops 1074790400 | bytes 6553600 | tf_op jit(solution)/shard_map/dot_general | solution.py:99
  179.5 67.3 %reduce-scatter.2.cloned.1.call-done = bf16[256,512]{1,0:T(8,128)(2,1)} async-done(((bf16[256,4096]{1,0:T(8,128)(2,1)}), bf16[256,512]{1,0:T(8,128)(2,1)}) %reduce-scatter.2.cloned.1.call-update) | async-done | bytes 262160 | tf_op jit(solution)/shard_map/reduce_scatter | solution.py:104
  (190 shorter events, 47.8 us)
Async XLA Ops:
  6.5 168.0 %all-gather.2.cloned.1.call-start = ((), (), s32[]{:S(2)}) async-start(), calls=%async_computation.1 | async-start | bytes 4259840 | tf_op jit(solution)/shard_map/all_gather | solution.py:101
  7.6 12.2 %collective-permute-start.16 = (bf16[256,512]{0,1:T(8,128)(2,1)S(1)}, bf16[256,512]{0,1:T(8,128)(2,1)S(1)}, u32[]{:S(2)}, u32[]{:S(2)}) collective-permute-start(bf16[256,512]{0,1:T(8,128)(2,1)S(1)} %copy.29), channel_id=1, source_target_pairs={{0,8},{8,16},{16,24},{24,32},{32,40},{40,48},{48,56},{56,64},{64,7... | collective-permute-start | bytes 786440 | tf_op jit(solution)/shard_map/ppermute | solution.py:15
  9.6 12.3 %collective-permute-start.24 = (bf16[256,512]{0,1:T(8,128)(2,1)S(1)}, bf16[256,512]{0,1:T(8,128)(2,1)S(1)}, u32[]{:S(2)}, u32[]{:S(2)}) collective-permute-start(bf16[256,512]{0,1:T(8,128)(2,1)S(1)} %copy.29), channel_id=1, source_target_pairs={{8,0},{16,8},{24,16},{32,24},{40,32},{48,40},{56,48},{64,56},{72,6... | collective-permute-start | bytes 786440 | tf_op jit(solution)/shard_map/ppermute | solution.py:15
  14.3 11.2 %collective-permute-start = (bf16[256,512]{0,1:T(8,128)(2,1)S(1)}, bf16[256,512]{0,1:T(8,128)(2,1)S(1)}, u32[]{:S(2)}, u32[]{:S(2)}) collective-permute-start(bf16[256,512]{0,1:T(8,128)(2,1)S(1)} %copy.25), channel_id=1, source_target_pairs={{0,8},{8,16},{16,24},{24,32},{32,40},{40,48},{48,56},{56,64},{64,7... | collective-permute-start | bytes 786440 | tf_op jit(solution)/shard_map/ppermute | solution.py:15
  16.2 11.2 %collective-permute-start.8 = (bf16[256,512]{0,1:T(8,128)(2,1)S(1)}, bf16[256,512]{0,1:T(8,128)(2,1)S(1)}, u32[]{:S(2)}, u32[]{:S(2)}) collective-permute-start(bf16[256,512]{0,1:T(8,128)(2,1)S(1)} %copy.25), channel_id=1, source_target_pairs={{8,0},{16,8},{24,16},{32,24},{40,32},{48,40},{56,48},{64,56},{72,6... | collective-permute-start | bytes 786440 | tf_op jit(solution)/shard_map/ppermute | solution.py:15
  19.9 11.2 %collective-permute-start.17 = (bf16[256,512]{0,1:T(8,128)(2,1)S(1)}, bf16[256,512]{0,1:T(8,128)(2,1)}, u32[]{:S(2)}, u32[]{:S(2)}) collective-permute-start(bf16[256,512]{0,1:T(8,128)(2,1)S(1)} %collective-permute-done.16), channel_id=1, source_target_pairs={{0,8},{8,16},{16,24},{24,32},{32,40},{40,48},{48,56},{56,64},{64,7... | collective-permute-start | bytes 786440 | tf_op jit(solution)/shard_map/ppermute | solution.py:15
  21.8 11.8 %collective-permute-start.25 = (bf16[256,512]{0,1:T(8,128)(2,1)S(1)}, bf16[256,512]{0,1:T(8,128)(2,1)S(1)}, u32[]{:S(2)}, u32[]{:S(2)}) collective-permute-start(bf16[256,512]{0,1:T(8,128)(2,1)S(1)} %collective-permute-done.24), channel_id=1, source_target_pairs={{8,0},{16,8},{24,16},{32,24},{40,32},{48,40},{56,48},{64,56},{72,6... | collective-permute-start | bytes 786440 | tf_op jit(solution)/shard_map/ppermute | solution.py:15
  25.5 11.2 %collective-permute-start.1 = (bf16[256,512]{0,1:T(8,128)(2,1)S(1)}, bf16[256,512]{0,1:T(8,128)(2,1)S(1)}, u32[]{:S(2)}, u32[]{:S(2)}) collective-permute-start(bf16[256,512]{0,1:T(8,128)(2,1)S(1)} %collective-permute-done), channel_id=1, source_target_pairs={{0,8},{8,16},{16,24},{24,32},{32,40},{40,48},{48,56},{56,64},{64,7... | collective-permute-start | bytes 786440 | tf_op jit(solution)/shard_map/ppermute | solution.py:15
  27.4 13.0 %collective-permute-start.9 = (bf16[256,512]{0,1:T(8,128)(2,1)S(1)}, bf16[256,512]{0,1:T(8,128)(2,1)S(1)}, u32[]{:S(2)}, u32[]{:S(2)}) collective-permute-start(bf16[256,512]{0,1:T(8,128)(2,1)S(1)} %collective-permute-done.8), channel_id=1, source_target_pairs={{8,0},{16,8},{24,16},{32,24},{40,32},{48,40},{56,48},{64,56},{72,6... | collective-permute-start | bytes 786440 | tf_op jit(solution)/shard_map/ppermute | solution.py:15
  31.1 11.3 %collective-permute-start.18 = (bf16[256,512]{0,1:T(8,128)(2,1)}, bf16[256,512]{0,1:T(8,128)(2,1)S(1)}, u32[]{:S(2)}, u32[]{:S(2)}) collective-permute-start(bf16[256,512]{0,1:T(8,128)(2,1)} %collective-permute-done.17), channel_id=1, source_target_pairs={{0,8},{8,16},{16,24},{24,32},{32,40},{40,48},{48,56},{56,64},{64,7... | collective-permute-start | bytes 786440 | tf_op jit(solution)/shard_map/ppermute | solution.py:15
  33.6 34.1 %copy-start.4 = (bf16[256,512]{0,1:T(8,128)(2,1)}, bf16[256,512]{0,1:T(8,128)(2,1)S(1)}, u32[]{:S(2)}) copy-start(bf16[256,512]{0,1:T(8,128)(2,1)S(1)} %collective-permute-done.25) | copy-start | bytes 786436
  33.6 13.6 %collective-permute-start.26 = (bf16[256,512]{0,1:T(8,128)(2,1)S(1)}, bf16[256,512]{0,1:T(8,128)(2,1)S(1)}, u32[]{:S(2)}, u32[]{:S(2)}) collective-permute-start(bf16[256,512]{0,1:T(8,128)(2,1)S(1)} %collective-permute-done.25), channel_id=1, source_target_pairs={{8,0},{16,8},{24,16},{32,24},{40,32},{48,40},{56,48},{64,56},{72,6... | collective-permute-start | bytes 786440 | tf_op jit(solution)/shard_map/ppermute | solution.py:15
  36.7 12.5 %collective-permute-start.2 = (bf16[256,512]{0,1:T(8,128)(2,1)S(1)}, bf16[256,512]{0,1:T(8,128)(2,1)S(1)}, u32[]{:S(2)}, u32[]{:S(2)}) collective-permute-start(bf16[256,512]{0,1:T(8,128)(2,1)S(1)} %collective-permute-done.1), channel_id=1, source_target_pairs={{0,8},{8,16},{16,24},{24,32},{32,40},{40,48},{48,56},{56,64},{64,7... | collective-permute-start | bytes 786440 | tf_op jit(solution)/shard_map/ppermute | solution.py:15
  40.4 13.6 %collective-permute-start.10 = (bf16[256,512]{0,1:T(8,128)(2,1)S(1)}, bf16[256,512]{0,1:T(8,128)(2,1)S(1)}, u32[]{:S(2)}, u32[]{:S(2)}) collective-permute-start(bf16[256,512]{0,1:T(8,128)(2,1)S(1)} %collective-permute-done.9), channel_id=1, source_target_pairs={{8,0},{16,8},{24,16},{32,24},{40,32},{48,40},{56,48},{64,56},{72,6... | collective-permute-start | bytes 786440 | tf_op jit(solution)/shard_map/ppermute | solution.py:15
  42.4 27.3 %copy-start.14 = (bf16[256,512]{0,1:T(8,128)(2,1)}, bf16[256,512]{0,1:T(8,128)(2,1)S(1)}, u32[]{:S(2)}) copy-start(bf16[256,512]{0,1:T(8,128)(2,1)S(1)} %collective-permute-done.18) | copy-start | bytes 786436
  42.4 13.6 %collective-permute-start.19 = (bf16[256,512]{0,1:T(8,128)(2,1)S(1)}, bf16[256,512]{0,1:T(8,128)(2,1)S(1)}, u32[]{:S(2)}, u32[]{:S(2)}) collective-permute-start(bf16[256,512]{0,1:T(8,128)(2,1)S(1)} %collective-permute-done.18), channel_id=1, source_target_pairs={{0,8},{8,16},{16,24},{24,32},{32,40},{40,48},{48,56},{56,64},{64,7... | collective-permute-start | bytes 786440 | tf_op jit(solution)/shard_map/ppermute | solution.py:15
  47.3 22.4 %copy-start.10 = (bf16[256,512]{0,1:T(8,128)(2,1)}, bf16[256,512]{0,1:T(8,128)(2,1)S(1)}, u32[]{:S(2)}) copy-start(bf16[256,512]{0,1:T(8,128)(2,1)S(1)} %collective-permute-done.26) | copy-start | bytes 786436
  47.3 13.6 %collective-permute-start.27 = (bf16[256,512]{0,1:T(8,128)(2,1)S(1)}, bf16[256,512]{0,1:T(8,128)(2,1)}, u32[]{:S(2)}, u32[]{:S(2)}) collective-permute-start(bf16[256,512]{0,1:T(8,128)(2,1)S(1)} %collective-permute-done.26), channel_id=1, source_target_pairs={{8,0},{16,8},{24,16},{32,24},{40,32},{48,40},{56,48},{64,56},{72,6... | collective-permute-start | bytes 786440 | tf_op jit(solution)/shard_map/ppermute | solution.py:15
  49.2 54.5 %copy-start.2 = (bf16[256,512]{0,1:T(8,128)(2,1)}, bf16[256,512]{0,1:T(8,128)(2,1)S(1)}, u32[]{:S(2)}) copy-start(bf16[256,512]{0,1:T(8,128)(2,1)S(1)} %collective-permute-done.2) | copy-start | bytes 786436
  49.2 13.6 %collective-permute-start.3 = (bf16[256,512]{0,1:T(8,128)(2,1)S(1)}, bf16[256,512]{0,1:T(8,128)(2,1)S(1)}, u32[]{:S(2)}, u32[]{:S(2)}) collective-permute-start(bf16[256,512]{0,1:T(8,128)(2,1)S(1)} %collective-permute-done.2), channel_id=1, source_target_pairs={{0,8},{8,16},{16,24},{24,32},{32,40},{40,48},{48,56},{56,64},{64,7... | collective-permute-start | bytes 786440 | tf_op jit(solution)/shard_map/ppermute | solution.py:15
  54.1 13.6 %collective-permute-start.11 = (bf16[256,512]{0,1:T(8,128)(2,1)S(1)}, bf16[256,512]{0,1:T(8,128)(2,1)S(1)}, u32[]{:S(2)}, u32[]{:S(2)}) collective-permute-start(bf16[256,512]{0,1:T(8,128)(2,1)S(1)} %collective-permute-done.10), channel_id=1, source_target_pairs={{8,0},{16,8},{24,16},{32,24},{40,32},{48,40},{56,48},{64,56},{72,6... | collective-permute-start | bytes 786440 | tf_op jit(solution)/shard_map/ppermute | solution.py:15
  56.0 13.7 %copy-start.15 = (bf16[256,512]{0,1:T(8,128)(2,1)}, bf16[256,512]{0,1:T(8,128)(2,1)S(1)}, u32[]{:S(2)}) copy-start(bf16[256,512]{0,1:T(8,128)(2,1)S(1)} %collective-permute-done.19) | copy-start | bytes 786436
  56.0 13.7 %collective-permute-start.20 = (bf16[256,512]{0,1:T(8,128)(2,1)S(1)}, bf16[256,512]{0,1:T(8,128)(2,1)}, u32[]{:S(2)}, u32[]{:S(2)}) collective-permute-start(bf16[256,512]{0,1:T(8,128)(2,1)S(1)} %collective-permute-done.19), channel_id=1, source_target_pairs={{0,8},{8,16},{16,24},{24,32},{32,40},{40,48},{48,56},{56,64},{64,7... | collective-permute-start | bytes 786440 | tf_op jit(solution)/shard_map/ppermute | solution.py:15
  60.9 13.8 %collective-permute-start.28 = (bf16[256,512]{0,1:T(8,128)(2,1)}, bf16[256,512]{0,1:T(8,128)(2,1)}, u32[]{:S(2)}, u32[]{:S(2)}) collective-permute-start(bf16[256,512]{0,1:T(8,128)(2,1)} %collective-permute-done.27), channel_id=1, source_target_pairs={{8,0},{16,8},{24,16},{32,24},{40,32},{48,40},{56,48},{64,56},{72,6... | collective-permute-start | bytes 786440 | tf_op jit(solution)/shard_map/ppermute | solution.py:15
  62.8 40.8 %copy-start.8 = (bf16[256,512]{0,1:T(8,128)(2,1)}, bf16[256,512]{0,1:T(8,128)(2,1)S(1)}, u32[]{:S(2)}) copy-start(bf16[256,512]{0,1:T(8,128)(2,1)S(1)} %collective-permute-done.3) | copy-start | bytes 786436
  62.9 13.7 %collective-permute-start.4 = (bf16[256,512]{0,1:T(8,128)(2,1)S(1)}, bf16[256,512]{0,1:T(8,128)(2,1)}, u32[]{:S(2)}, u32[]{:S(2)}) collective-permute-start(bf16[256,512]{0,1:T(8,128)(2,1)S(1)} %collective-permute-done.3), channel_id=1, source_target_pairs={{0,8},{8,16},{16,24},{24,32},{32,40},{40,48},{48,56},{56,64},{64,7... | collective-permute-start | bytes 786440 | tf_op jit(solution)/shard_map/ppermute | solution.py:15
  67.7 37.1 %copy-start.6 = (bf16[256,512]{0,1:T(8,128)(2,1)}, bf16[256,512]{0,1:T(8,128)(2,1)S(1)}, u32[]{:S(2)}) copy-start(bf16[256,512]{0,1:T(8,128)(2,1)S(1)} %collective-permute-done.11) | copy-start | bytes 786436
  67.7 13.7 %collective-permute-start.12 = (bf16[256,512]{0,1:T(8,128)(2,1)S(1)}, bf16[256,512]{0,1:T(8,128)(2,1)S(1)}, u32[]{:S(2)}, u32[]{:S(2)}) collective-permute-start(bf16[256,512]{0,1:T(8,128)(2,1)S(1)} %collective-permute-done.11), channel_id=1, source_target_pairs={{8,0},{16,8},{24,16},{32,24},{40,32},{48,40},{56,48},{64,56},{72,6... | collective-permute-start | bytes 786440 | tf_op jit(solution)/shard_map/ppermute | solution.py:15
  69.7 13.7 %collective-permute-start.21 = (bf16[256,512]{0,1:T(8,128)(2,1)}, bf16[256,512]{0,1:T(8,128)(2,1)}, u32[]{:S(2)}, u32[]{:S(2)}) collective-permute-start(bf16[256,512]{0,1:T(8,128)(2,1)} %collective-permute-done.20), channel_id=1, source_target_pairs={{0,8},{8,16},{16,24},{24,32},{32,40},{40,48},{48,56},{56,64},{64,7... | collective-permute-start | bytes 786440 | tf_op jit(solution)/shard_map/ppermute | solution.py:15
  74.6 172.1 %reduce-scatter.2.cloned.1.call-start = ((), (), s32[]{:S(2)}) async-start(), calls=%async_computation.2 | async-start | bytes 2359296 | tf_op jit(solution)/shard_map/reduce_scatter | solution.py:104
  74.7 15.3 %collective-permute-start.29 = (bf16[256,512]{0,1:T(8,128)(2,1)}, bf16[256,512]{0,1:T(8,128)(2,1)}, u32[]{:S(2)}, u32[]{:S(2)}) collective-permute-start(bf16[256,512]{0,1:T(8,128)(2,1)} %collective-permute-done.28), channel_id=1, source_target_pairs={{8,0},{16,8},{24,16},{32,24},{40,32},{48,40},{56,48},{64,56},{72,6... | collective-permute-start | bytes 786440 | tf_op jit(solution)/shard_map/ppermute | solution.py:15
  76.6 15.3 %collective-permute-start.5 = (bf16[256,512]{0,1:T(8,128)(2,1)}, bf16[256,512]{0,1:T(8,128)(2,1)}, u32[]{:S(2)}, u32[]{:S(2)}) collective-permute-start(bf16[256,512]{0,1:T(8,128)(2,1)} %collective-permute-done.4), channel_id=1, source_target_pairs={{0,8},{8,16},{16,24},{24,32},{32,40},{40,48},{48,56},{56,64},{64,7... | collective-permute-start | bytes 786440 | tf_op jit(solution)/shard_map/ppermute | solution.py:15
  81.5 22.1 %copy-start.12 = (bf16[256,512]{0,1:T(8,128)(2,1)}, bf16[256,512]{0,1:T(8,128)(2,1)S(1)}, u32[]{:S(2)}) copy-start(bf16[256,512]{0,1:T(8,128)(2,1)S(1)} %collective-permute-done.12) | copy-start | bytes 786436
  81.5 15.3 %collective-permute-start.13 = (bf16[256,512]{0,1:T(8,128)(2,1)S(1)}, bf16[256,512]{0,1:T(8,128)(2,1)}, u32[]{:S(2)}, u32[]{:S(2)}) collective-permute-start(bf16[256,512]{0,1:T(8,128)(2,1)S(1)} %collective-permute-done.12), channel_id=1, source_target_pairs={{8,0},{16,8},{24,16},{32,24},{40,32},{48,40},{56,48},{64,56},{72,6... | collective-permute-start | bytes 786440 | tf_op jit(solution)/shard_map/ppermute | solution.py:15
  83.4 15.3 %collective-permute-start.22 = (bf16[256,512]{0,1:T(8,128)(2,1)}, bf16[256,512]{0,1:T(8,128)(2,1)}, u32[]{:S(2)}, u32[]{:S(2)}) collective-permute-start(bf16[256,512]{0,1:T(8,128)(2,1)} %collective-permute-done.21), channel_id=1, source_target_pairs={{0,8},{8,16},{16,24},{24,32},{32,40},{40,48},{48,56},{56,64},{64,7... | collective-permute-start | bytes 786440 | tf_op jit(solution)/shard_map/ppermute | solution.py:15
  90.0 16.4 %collective-permute-start.30 = (bf16[256,512]{0,1:T(8,128)(2,1)}, bf16[256,512]{0,1:T(8,128)(2,1)}, u32[]{:S(2)}, u32[]{:S(2)}) collective-permute-start(bf16[256,512]{0,1:T(8,128)(2,1)} %collective-permute-done.29), channel_id=1, source_target_pairs={{8,0},{16,8},{24,16},{32,24},{40,32},{48,40},{56,48},{64,56},{72,6... | collective-permute-start | bytes 786440 | tf_op jit(solution)/shard_map/ppermute | solution.py:15
  91.9 16.4 %collective-permute-start.6 = (bf16[256,512]{0,1:T(8,128)(2,1)}, bf16[256,512]{0,1:T(8,128)(2,1)}, u32[]{:S(2)}, u32[]{:S(2)}) collective-permute-start(bf16[256,512]{0,1:T(8,128)(2,1)} %collective-permute-done.5), channel_id=1, source_target_pairs={{0,8},{8,16},{16,24},{24,32},{32,40},{40,48},{48,56},{56,64},{64,7... | collective-permute-start | bytes 786440 | tf_op jit(solution)/shard_map/ppermute | solution.py:15
  96.8 16.4 %collective-permute-start.14 = (bf16[256,512]{0,1:T(8,128)(2,1)}, bf16[256,512]{0,1:T(8,128)(2,1)}, u32[]{:S(2)}, u32[]{:S(2)}) collective-permute-start(bf16[256,512]{0,1:T(8,128)(2,1)} %collective-permute-done.13), channel_id=1, source_target_pairs={{8,0},{16,8},{24,16},{32,24},{40,32},{48,40},{56,48},{64,56},{72,6... | collective-permute-start | bytes 786440 | tf_op jit(solution)/shard_map/ppermute | solution.py:15
  98.7 16.4 %collective-permute-start.23 = (bf16[256,512]{0,1:T(8,128)(2,1)}, bf16[256,512]{0,1:T(8,128)(2,1)}, u32[]{:S(2)}, u32[]{:S(2)}) collective-permute-start(bf16[256,512]{0,1:T(8,128)(2,1)} %collective-permute-done.22), channel_id=1, source_target_pairs={{0,8},{8,16},{16,24},{24,32},{32,40},{40,48},{48,56},{56,64},{64,7... | collective-permute-start | bytes 786440 | tf_op jit(solution)/shard_map/ppermute | solution.py:15
  105.0 17.1 %copy-start.5 = (bf16[256,512]{0,1:T(8,128)(2,1)S(1)}, bf16[256,512]{0,1:T(8,128)(2,1)}, u32[]{:S(2)}) copy-start(bf16[256,512]{0,1:T(8,128)(2,1)} %copy-done.4) | copy-start | bytes 786436
  105.0 17.2 %copy-start.11 = (bf16[256,512]{0,1:T(8,128)(2,1)S(1)}, bf16[256,512]{0,1:T(8,128)(2,1)}, u32[]{:S(2)}) copy-start(bf16[256,512]{0,1:T(8,128)(2,1)} %copy-done.10) | copy-start | bytes 786436
  106.4 19.8 %collective-permute-start.31 = (bf16[256,512]{0,1:T(8,128)(2,1)}, bf16[256,512]{0,1:T(8,128)(2,1)S(1)}, u32[]{:S(2)}, u32[]{:S(2)}) collective-permute-start(bf16[256,512]{0,1:T(8,128)(2,1)} %collective-permute-done.30), channel_id=1, source_target_pairs={{8,0},{16,8},{24,16},{32,24},{40,32},{48,40},{56,48},{64,56},{72,6... | collective-permute-start | bytes 786440 | tf_op jit(solution)/shard_map/ppermute | solution.py:15
  108.4 17.9 %collective-permute-start.7 = (bf16[256,512]{0,1:T(8,128)(2,1)}, bf16[256,512]{0,1:T(8,128)(2,1)S(1)}, u32[]{:S(2)}, u32[]{:S(2)}) collective-permute-start(bf16[256,512]{0,1:T(8,128)(2,1)} %collective-permute-done.6), channel_id=1, source_target_pairs={{0,8},{8,16},{16,24},{24,32},{32,40},{40,48},{48,56},{56,64},{64,7... | collective-permute-start | bytes 786440 | tf_op jit(solution)/shard_map/ppermute | solution.py:15
  113.2 18.7 %collective-permute-start.15 = (bf16[256,512]{0,1:T(8,128)(2,1)}, bf16[256,512]{0,1:T(8,128)(2,1)S(1)}, u32[]{:S(2)}, u32[]{:S(2)}) collective-permute-start(bf16[256,512]{0,1:T(8,128)(2,1)} %collective-permute-done.14), channel_id=1, source_target_pairs={{8,0},{16,8},{24,16},{32,24},{40,32},{48,40},{56,48},{64,56},{72,6... | collective-permute-start | bytes 786440 | tf_op jit(solution)/shard_map/ppermute | solution.py:15
  119.1 10.6 %copy-start.9 = (bf16[256,512]{0,1:T(8,128)(2,1)S(1)}, bf16[256,512]{0,1:T(8,128)(2,1)}, u32[]{:S(2)}) copy-start(bf16[256,512]{0,1:T(8,128)(2,1)} %copy-done.8) | copy-start | bytes 786436
  120.1 9.6 %copy-start.3 = (bf16[256,512]{0,1:T(8,128)(2,1)S(1)}, bf16[256,512]{0,1:T(8,128)(2,1)}, u32[]{:S(2)}) copy-start(bf16[256,512]{0,1:T(8,128)(2,1)} %copy-done.2) | copy-start | bytes 786436
  122.2 7.7 %copy-start.7 = (bf16[256,512]{0,1:T(8,128)(2,1)S(1)}, bf16[256,512]{0,1:T(8,128)(2,1)}, u32[]{:S(2)}) copy-start(bf16[256,512]{0,1:T(8,128)(2,1)} %copy-done.6) | copy-start | bytes 786436
  123.3 6.7 %copy-start.13 = (bf16[256,512]{0,1:T(8,128)(2,1)S(1)}, bf16[256,512]{0,1:T(8,128)(2,1)}, u32[]{:S(2)}) copy-start(bf16[256,512]{0,1:T(8,128)(2,1)} %copy-done.12) | copy-start | bytes 786436
  (2 other events, 7.9 us)
Sparse Core Ops, SparseCore 0:
  74.7 99.7 all-gather.1
  179.6 67.0 reduce-scatter.1
where the time goes:
time: 256 us; the launch traced here: 254 us
  starting transfers between devices  101 us (39%)
  waiting for transfers between devices  67.4 us (26%)
  local copies, waits for them, and re-layouts  41.5 us (16%)
  matrix products  19.7 us (8%)
  between operations  14.4 us (6%)
  other arithmetic  8.77 us (3%)
    ppermute x32, starting transfers between devices, passed_along(): lax.ppermute(value, axis, [(source, source + steps) for source in range(f...  101 us
    reduce_scatter x1, waiting for transfers between devices, local(): lax.psum_scatter(partial_value.astype(jnp.bfloat16), 'tp', scatter_dimens...  67.3 us
    unnamed x70, local copies, waits for them, and re-layouts  22.1 us
    dynamic_slice x9, local copies, waits for them, and re-layouts, step_window(): block_values = lax.dynamic_slice_in_dim(window_values, offset, span, 0)  11.6 us
    dot_general x9, matrix products, absorb(): jnp.einsum('hqk,khd->hqd', weights.astype(jnp.bfloat16), value_heads, pre...  9.73 us
    dynamic_slice x9, local copies, waits for them, and re-layouts, step_window(): block_ids = lax.dynamic_slice_in_dim(window_ids, offset, span, 0)  6.79 us
    dot_general x9, matrix products, absorb(): jnp.einsum('qhd,khd->hqk', query_heads, key_heads, preferred_element_type...  5.14 us
  transfers between devices with their start and end apart: 34, of which 1 were waited for; matrix products, arithmetic and copies ran while one was open for 24% of the time, Pallas kernels for 0%

commit v1 on v0

v1 whole, which is shorter than its diff:
```python
import functools
import math

import jax
import jax.numpy as jnp
from jax import lax
from jax.experimental import pallas as pl
from jax.experimental.pallas import tpu as pltpu
from jax.sharding import PartitionSpec as P


HD = 128
X, Y, Z = 4, 8, 8
HOPS = 4
LOW = -1e30
MASKED = -3e37
C2 = math.log2(math.e) / math.sqrt(HD)


def device(x, y, core):
    return ((x % X) * Y + y % Y) * 2 + core


def pairs_of(step):
    return [
        (device(x, y, core), device(*step(x, y, core)))
        for x in range(X)
        for y in range(Y)
        for core in range(2)
    ]


SWAP = pairs_of(lambda x, y, core: (x, y, 1 - core))
Y_WAYS = pairs_of(lambda x, y, core: (x, y + 1 - 2 * core, core))
X_FAR = {far: pairs_of(lambda x, y, core, far=far: (x + far, y, core)) for far in range(1, X)}
SIDES = [(s, s + 2 - 4 * (s % 2)) for s in range(2 * X * Y) if 0 <= s + 2 - 4 * (s % 2) < 2 * X * Y]
Z_UP = [(z, (z + 1) % Z) for z in range(Z)]
Z_DOWN = [(z, (z - 1) % Z) for z in range(Z)]
TURN = [
    ((8 * a + j) * Z + b, (8 * b + j) * Z + a) for a in range(Z) for b in range(Z) for j in range(8)
]


def attend_kernel(first, blocks, scal, bounds, q_own, q_par, *refs):
    count = len(blocks)
    kvs = refs[:count]
    if first:
        outs = refs[count:]
        for out in outs:
            out[0:512, :] = jnp.zeros((512, 256), jnp.float32)
            row = lax.broadcasted_iota(jnp.int32, (32, 256), 0)
            out[512:544, :] = jnp.where(row % 8 == 0, LOW, 0.0)
    else:
        ins = refs[count : count + 2]
        outs = refs[count + 2 :]
        for given, out in zip(ins, outs, strict=True):
            out[...] = given[...]

    for half, (q_ref, state) in enumerate(zip((q_own, q_par), outs, strict=True)):
        low_first, high_last = scal[16 + 4 * half], scal[19 + 4 * half]

        def tile(kv, start, half=half, q_ref=q_ref, state=state):
            wide = 256
            spot = lax.broadcasted_iota(jnp.int32, (256, wide), 0) + start
            jobs = [(head, part) for part in range(256 // wide) for head in range(4)]

            def score(job):
                head, part = job
                lanes = slice(head * HD, (head + 1) * HD)
                return lax.dot_general(
                    kv[0:256, lanes],
                    q_ref[part * wide : (part + 1) * wide, lanes],
                    (((1,), (1,)), ((), ())),
                    preferred_element_type=jnp.float32,
                )

            keeps = []
            for part in range(256 // wide):
                columns = slice(part * wide, (part + 1) * wide)
                keeps.append(
                    (spot >= bounds[2 * half : 2 * half + 1, columns])
                    & (spot < bounds[2 * half + 1 : 2 * half + 2, columns])
                )
            ahead = {number: score(jobs[number]) for number in range(2)}
            for number, (head, part) in enumerate(jobs):
                columns = slice(part * wide, (part + 1) * wide)
                lanes = slice(head * HD, (head + 1) * HD)
                stats = slice(512 + 8 * head, 520 + 8 * head)
                if number + 2 < len(jobs):
                    ahead[number + 2] = score(jobs[number + 2])
                scores = jnp.where(keeps[part], ahead.pop(number), MASKED)
                held = state[stats, columns]
                old = held[0:1, :]
                new = jnp.maximum(old, jnp.max(scores, axis=0, keepdims=True))
                weights = jnp.exp2(scores * C2 - new * C2)
                factor = jnp.exp2((old - new) * C2)
                total = held[1:2, :] * factor + jnp.sum(weights, axis=0, keepdims=True)
                mixed = lax.dot_general(
                    kv[256:512, lanes],
                    weights.astype(jnp.bfloat16),
                    (((0,), (0,)), ((), ())),
                    preferred_element_type=jnp.float32,
                )
                state[stats, columns] = jnp.concatenate([new, total, held[2:8, :]], axis=0)
                state[lanes, columns] = state[lanes, columns] * factor + mixed

        for kv, number in zip(kvs, blocks, strict=True):
            start = scal[number]
            touches = (start < high_last) & (start + 256 > low_first)

            @pl.when(touches)
            def _(kv=kv, start=start, tile=tile):
                tile(kv, start)


def attend(scal, bounds, q_own, q_par, kvs, blocks, states):
    vmem = pl.BlockSpec(memory_space=pltpu.VMEM)
    first = states is None
    given = () if first else states
    state = jax.ShapeDtypeStruct((544, 256), jnp.float32)
    pairs = 256 * 512 * 4 * len(kvs)
    before = 4 + len(kvs)
    return pl.pallas_call(
        functools.partial(attend_kernel, first, tuple(blocks)),
        out_shape=(state, state),
        in_specs=[pl.BlockSpec(memory_space=pltpu.SMEM)] + [vmem] * (3 + len(kvs) + len(given)),
        out_specs=(vmem, vmem),
        input_output_aliases={} if first else {before: 0, before + 1: 1},
        cost_estimate=pl.CostEstimate(
            flops=4 * pairs * HD, bytes_accessed=1 << 20, transcendentals=pairs
        ),
        compiler_params=pltpu.CompilerParams(vmem_limit_bytes=24 << 20),
        name="attend",
    )(scal, bounds, q_own, q_par, *kvs, *given)


def pack_kernel(top, bottom, out, sems):
    copies = [
        pltpu.make_async_copy(ref, out.at[pl.ds(256 * half, 256)], sems.at[half])
        for half, ref in enumerate((top, bottom))
    ]
    for copy in copies:
        copy.start()
    for copy in copies:
        copy.wait()


def pack(top, bottom):
    return pl.pallas_call(
        pack_kernel,
        out_shape=jax.ShapeDtypeStruct((512, 512), jnp.bfloat16),
        in_specs=[pl.BlockSpec(memory_space=pl.ANY)] * 2,
        out_specs=pl.BlockSpec(memory_space=pltpu.VMEM),
        scratch_shapes=[pltpu.SemaphoreType.DMA((2,))],
        cost_estimate=pl.CostEstimate(flops=0, bytes_accessed=1 << 20, transcendentals=0),
        compiler_params=pltpu.CompilerParams(vmem_limit_bytes=4 << 20),
        name="pack",
    )(top, bottom)


def merge_kernel(mine, other, out):
    for head in range(4):
        at = 512 + 8 * head
        top_a, top_b = mine[at : at + 1, :], other[at : at + 1, :]
        top = jnp.maximum(top_a, top_b)
        f_a, f_b = jnp.exp2((top_a - top) * C2), jnp.exp2((top_b - top) * C2)
        total = mine[at + 1 : at + 2, :] * f_a + other[at + 1 : at + 2, :] * f_b
        rows = slice(head * HD, (head + 1) * HD)
        mixed = (mine[rows, :] * f_a + other[rows, :] * f_b) / total
        out[:, rows] = jnp.transpose(mixed).astype(jnp.bfloat16)


def merge(mine, other):
    vmem = pl.BlockSpec(memory_space=pltpu.VMEM)
    return pl.pallas_call(
        merge_kernel,
        out_shape=jax.ShapeDtypeStruct((256, 512), jnp.bfloat16),
        in_specs=[vmem, vmem],
        out_specs=vmem,
        cost_estimate=pl.CostEstimate(flops=1 << 20, bytes_accessed=1 << 20, transcendentals=4096),
        compiler_params=pltpu.CompilerParams(vmem_limit_bytes=8 << 20),
        name="merge",
    )(mine, other)


def arrange_kernel(scal, *refs):
    out = refs[-1]
    x, y, core, z = scal[24], scal[25], scal[26], scal[27]
    way = 1 - 2 * core
    for number, far in enumerate((0, -1, -2, -3, -4, 1, 2, 3)):
        yy = (y + Y + way * far) % Y
        column = pl.multiple_of((yy % 4) * 128, 128)
        for i in range(X):
            xx = (x + X - i) % X
            slot = (z + Z - (2 * xx + yy // 4)) % Z
            out[slot, pl.ds(column, 128), :] = refs[number][i]


def arrange(scal, groups):
    vmem = pl.BlockSpec(memory_space=pltpu.VMEM)
    return pl.pallas_call(
        arrange_kernel,
        out_shape=jax.ShapeDtypeStruct((Z, 512, 512), jnp.bfloat16),
        in_specs=[pl.BlockSpec(memory_space=pltpu.SMEM)] + [vmem] * len(groups),
        out_specs=vmem,
        cost_estimate=pl.CostEstimate(flops=0, bytes_accessed=8 << 20, transcendentals=0),
        compiler_params=pltpu.CompilerParams(vmem_limit_bytes=16 << 20),
        name="arrange",
    )(scal, *groups)


def project_kernel(slots, partial, *refs):
    count = len(slots)
    weight, out = refs[count], refs[-1]
    total = refs[count + 1][...] if partial else None
    for ref, slot in zip(refs[:count], slots, strict=True):
        term = lax.dot_general(
            ref[...],
            weight[slot],
            (((1,), (1,)), ((), ())),
            preferred_element_type=jnp.float32,
        )
        total = term if total is None else total + term
    out[...] = total.astype(out.dtype)


def project(blocks, slots, weight, partial, last):
    vmem = pl.BlockSpec(memory_space=pltpu.VMEM)
    given = () if partial is None else (partial,)
    return pl.pallas_call(
        functools.partial(project_kernel, tuple(slots), partial is not None),
        out_shape=jax.ShapeDtypeStruct((256, 512), jnp.bfloat16 if last else jnp.float32),
        in_specs=[vmem] * (len(blocks) + 1 + len(given)),
        out_specs=vmem,
        cost_estimate=pl.CostEstimate(
            flops=2 * 256 * 512 * 512 * len(blocks), bytes_accessed=6 << 20, transcendentals=0
        ),
        compiler_params=pltpu.CompilerParams(vmem_limit_bytes=16 << 20),
        name="project",
    )(*blocks, weight, *given)


def local(queries, keys, values, doc_lengths, out_weight):
    s = lax.axis_index("seq").astype(jnp.int32)
    z = lax.axis_index("tp").astype(jnp.int32)
    core, chip = s % 2, s // 2
    rows = queries.shape[0]

    ends = jnp.cumsum(doc_lengths)
    spots = (chip * 2 + jnp.stack([core, 1 - core]))[:, None] * rows + jnp.arange(rows, dtype=jnp.int32)
    ended = ends[:, None, None] <= spots[None]
    low = jnp.max(jnp.where(ended, ends[:, None, None], 0), axis=0)
    high = jnp.min(jnp.where(ended, jnp.int32(1 << 30), ends[:, None, None]), axis=0)
    bounds = jnp.stack([low[0], high[0], low[1], high[1]])
    bounds = jnp.concatenate([bounds, bounds], axis=0)
    way = 1 - 2 * core
    starts = [s * rows]
    for hop in range(1, HOPS + 1):
        there = 2 * (chip - way * hop)
        starts += [(there + core) * rows, (there + 1 - core) * rows]
    starts = jnp.stack(starts + [jnp.int32(0)] * 7)
    edges = jnp.stack([low[:, 0], low[:, -1], high[:, 0], high[:, -1]], axis=1).reshape(8)
    place = jnp.stack([chip // Y, chip % Y, core, z] + [jnp.int32(0)] * 4)
    scal = jnp.concatenate([starts, edges, place])

    mine = pack(keys, values)
    own_chain, par_chain = [mine], [lax.ppermute(mine, "seq", SWAP)]
    q_par = lax.ppermute(queries, "seq", SWAP)
    for _ in range(1, HOPS + 1):
        own_chain.append(lax.ppermute(own_chain[-1], "seq", SIDES))
        par_chain.append(lax.ppermute(par_chain[-1], "seq", SIDES))
    states = None
    for hop in range(HOPS + 1):
        kvs = [mine] if hop == 0 else [own_chain[hop], par_chain[hop]]
        blocks = (0,) if hop == 0 else (2 * hop - 1, 2 * hop)
        states = attend(scal, bounds, queries, q_par, kvs, blocks, states)

    piece = lax.ppermute(out_weight.T, ("seq", "tp"), TURN)
    beside = lax.ppermute(piece, "seq", SWAP)
    piece = jnp.where(
        core == 0,
        jnp.concatenate([piece, beside], axis=0),
        jnp.concatenate([beside, piece], axis=0),
    )
    line = [piece]
    for far in range(1, X):
        line.append(lax.ppermute(piece, "seq", X_FAR[far]))
    groups = [jnp.stack(line)]
    for _ in range(1, 5):
        groups.append(lax.ppermute(groups[-1], "seq", Y_WAYS))
    groups += [lax.ppermute(groups[far], "seq", SWAP) for far in range(1, 4)]
    weight = arrange(scal, groups)

    other = lax.ppermute(states[1], "seq", SWAP)
    attended = merge(states[0], other)
    up, down = [attended], [attended]
    for far in range(1, 5):
        up.append(lax.ppermute(up[-1], "tp", Z_UP))
        if far < 4:
            down.append(lax.ppermute(down[-1], "tp", Z_DOWN))
    partial = project(up[:4] + down[1:3], (0, 1, 2, 3, 7, 6), weight, None, False)
    return project([up[4], down[3]], (4, 5), weight, partial, True)


def solution(mesh):
    in_specs = (P("seq", "tp"), P("seq", "tp"), P("seq", "tp"), P(), P("tp", "seq"))
    return jax.shard_map(
        local, mesh=mesh, in_specs=in_specs, out_specs=P("seq", "tp"), check_vma=False
    )
```

time: 256 us -> 163 us (0.64)
  the two profiles are of different devices: /device:TPU:16 before, /device:TPU:60 now
where the time goes in v1:
time: 163 us; the launch traced here: 162 us
  starting transfers between devices  105 us (64%)
  waiting for transfers between devices  31.2 us (19%)
  Pallas kernels  21.5 us (13%)
  local copies, waits for them, and re-layouts  3.88 us (2%)
    pallas_call x5, Pallas kernels, attend(): pl.pallas_call(functools.partial(attend_kernel, first, tuple(blocks)), ou...  18.2 us
    ppermute x3, starting transfers between devices, local(): down.append(lax.ppermute(down[-1], 'tp', Z_DOWN))  15.2 us
    ppermute x1, starting transfers between devices, local(): piece = lax.ppermute(out_weight.T, ('seq', 'tp'), TURN)  14.6 us
    ppermute x4, starting transfers between devices, local(): par_chain.append(lax.ppermute(par_chain[-1], 'seq', SIDES))  13.7 us
    ppermute x4, starting transfers between devices, local(): up.append(lax.ppermute(up[-1], 'tp', Z_UP))  13.1 us
    ppermute x4, starting transfers between devices, local(): groups.append(lax.ppermute(groups[-1], 'seq', Y_WAYS))  11.6 us
    ppermute x4, starting transfers between devices, local(): own_chain.append(lax.ppermute(own_chain[-1], 'seq', SIDES))  10.6 us
    ppermute x4, waiting for transfers between devices, local(): up.append(lax.ppermute(up[-1], 'tp', Z_UP))  9.88 us
  transfers between devices with their start and end apart: 30, of which 8 were waited for; matrix products, arithmetic and copies ran while one was open for 1% of the time, Pallas kernels for 13%

profile of v1, /device:TPU:60, one launch (start us, length us, event | category | flops | bytes accessed | tf_op | source)
XLA Modules:
  0.0 162.3 jit_solution(11645669516431876858)
XLA Ops:
  0.0 0.9 copy-done.1
  1.0 0.9 copy-done.2
  2.0 1.9 %collective-permute-start.5 = (bf16[512,512]{1,0:T(8,128)(2,1)S(1)}, bf16[512,512]{1,0:T(8,128)(2,1)S(1)}, u32[]{:S(2)}, u32[]{:S(2)}) collective-permute-start(bf16[512,512]{1,0:T(8,128)(2,1)S(1)} %pack.1.refs_0_), channel_id=1, source_target_pairs={{0,8},{8,0},{16,24},{24,16},{32,40},{40,32},{48,56},{56,48},{64,72... | collective-permute-start | bytes 1572872 | tf_op jit(solution)/shard_map/ppermute | solution.py:267
  3.9 2.3 %collective-permute-start.1 = (bf16[512,512]{1,0:T(8,128)(2,1)S(1)}, bf16[512,512]{1,0:T(8,128)(2,1)S(1)}, u32[]{:S(2)}, u32[]{:S(2)}) collective-permute-start(bf16[512,512]{1,0:T(8,128)(2,1)S(1)} %pack.1.refs_0_), channel_id=1, source_target_pairs={{0,16},{16,32},{24,8},{32,48},{40,24},{48,64},{56,40},{64,80},{72,... | collective-permute-start | bytes 1572872 | tf_op jit(solution)/shard_map/ppermute | solution.py:270
  6.2 3.5 %collective-permute-start.6 = (bf16[512,512]{1,0:T(8,128)(2,1)S(1)}, bf16[512,512]{1,0:T(8,128)(2,1)S(1)}, u32[]{:S(2)}, u32[]{:S(2)}) collective-permute-start(bf16[512,512]{1,0:T(8,128)(2,1)S(1)} %collective-permute-done.5), channel_id=1, source_target_pairs={{0,16},{16,32},{24,8},{32,48},{40,24},{48,64},{56,40},{64,80},{72,... | collective-permute-start | bytes 1572872 | tf_op jit(solution)/shard_map/ppermute | solution.py:271
  9.7 5.3 %collective-permute-done.1.refs_0_ = bf16[512,512]{1,0:T(8,128)(2,1)S(1)} collective-permute-done((bf16[512,512]{1,0:T(8,128)(2,1)S(1)}, bf16[512,512]{1,0:T(8,128)(2,1)S(1)}, u32[]{:S(2)}, u32[]{:S(2)}) %collective-permute-start.1) | collective-permute-done | bytes 524320 | tf_op jit(solution)/shard_map/ppermute | solution.py:270
  15.0 4.4 %collective-permute-start.2 = (bf16[512,512]{1,0:T(8,128)(2,1)S(1)}, bf16[512,512]{1,0:T(8,128)(2,1)S(1)}, u32[]{:S(2)}, u32[]{:S(2)}) collective-permute-start(bf16[512,512]{1,0:T(8,128)(2,1)S(1)} %collective-permute-done.1.refs_0_), channel_id=1, source_target_pairs={{0,16},{16,32},{24,8},{32,48},{40,24},{48,64},{56,40},{64,80},{72,... | collective-permute-start | bytes 1572872 | tf_op jit(solution)/shard_map/ppermute | solution.py:270
  19.4 1.2 collective-permute-done.6.refs_1_
  20.6 4.4 %collective-permute-start.7 = (bf16[512,512]{1,0:T(8,128)(2,1)S(1)}, bf16[512,512]{1,0:T(8,128)(2,1)}, u32[]{:S(2)}, u32[]{:S(2)}) collective-permute-start(bf16[512,512]{1,0:T(8,128)(2,1)S(1)} %collective-permute-done.6.refs_1_), channel_id=1, source_target_pairs={{0,16},{16,32},{24,8},{32,48},{40,24},{48,64},{56,40},{64,80},{72,... | collective-permute-start | bytes 1572872 | tf_op jit(solution)/shard_map/ppermute | solution.py:271
  25.0 14.6 %collective-permute-start.18 = (bf16[64,512]{1,0:T(8,128)(2,1)}, bf16[64,512]{1,0:T(8,128)(2,1)S(1)}, u32[]{:S(2)}, u32[]{:S(2)}) collective-permute-start(bf16[64,512]{1,0:T(8,128)(2,1)} %bitcast.27), channel_id=1, source_target_pairs={{0,0},{8,8},{16,16},{24,24},{32,32},{40,40},{48,48},{56,56},{1,64}... | collective-permute-start | bytes 196616 | tf_op jit(solution)/shard_map/ppermute | solution.py:278
  39.7 4.1 %collective-permute-done.18 = bf16[64,512]{1,0:T(8,128)(2,1)S(1)} collective-permute-done((bf16[64,512]{1,0:T(8,128)(2,1)}, bf16[64,512]{1,0:T(8,128)(2,1)S(1)}, u32[]{:S(2)}, u32[]{:S(2)}) %collective-permute-start.18) | collective-permute-done | bytes 65568 | tf_op jit(solution)/shard_map/ppermute | solution.py:278
  43.8 1.9 %collective-permute-start.19 = (bf16[64,512]{1,0:T(8,128)(2,1)S(1)}, bf16[64,512]{1,0:T(8,128)(2,1)S(1)}, u32[]{:S(2)}, u32[]{:S(2)}) collective-permute-start(bf16[64,512]{1,0:T(8,128)(2,1)S(1)} %collective-permute-done.18), channel_id=1, source_target_pairs={{0,8},{8,0},{16,24},{24,16},{32,40},{40,32},{48,56},{56,48},{64,72... | collective-permute-start | bytes 196616 | tf_op jit(solution)/shard_map/ppermute | solution.py:279
  45.7 1.9 %collective-permute-start.3 = (bf16[512,512]{1,0:T(8,128)(2,1)S(1)}, bf16[512,512]{1,0:T(8,128)(2,1)}, u32[]{:S(2)}, u32[]{:S(2)}) collective-permute-start(bf16[512,512]{1,0:T(8,128)(2,1)S(1)} %collective-permute-done.2.refs_0_), channel_id=1, source_target_pairs={{0,16},{16,32},{24,8},{32,48},{40,24},{48,64},{56,40},{64,80},{72,... | collective-permute-start | bytes 1572872 | tf_op jit(solution)/shard_map/ppermute | solution.py:270
  47.7 1.9 %collective-permute-start.8 = (bf16[512,512]{1,0:T(8,128)(2,1)}, bf16[512,512]{1,0:T(8,128)(2,1)}, u32[]{:S(2)}, u32[]{:S(2)}) collective-permute-start(bf16[512,512]{1,0:T(8,128)(2,1)} %collective-permute-done.7.refs_1_), channel_id=1, source_target_pairs={{0,16},{16,32},{24,8},{32,48},{40,24},{48,64},{56,40},{64,80},{72,... | collective-permute-start | bytes 1572872 | tf_op jit(solution)/shard_map/ppermute | solution.py:271
  50.6 1.9 %collective-permute-start.20 = (bf16[128,512]{1,0:T(8,128)(2,1)S(1)}, bf16[128,512]{1,0:T(8,128)(2,1)S(1)}, u32[]{:S(2)}, u32[]{:S(2)}) collective-permute-start(bf16[128,512]{1,0:T(8,128)(2,1)S(1)} %maximum_select_fusion.1), channel_id=1, source_target_pairs={{0,128},{8,136},{16,144},{24,152},{32,160},{40,168},{48,176},{56,1... | collective-permute-start | bytes 393224 | tf_op jit(solution)/shard_map/ppermute | solution.py:287
  52.5 1.9 %collective-permute-start.21 = (bf16[128,512]{1,0:T(8,128)(2,1)S(1)}, bf16[128,512]{1,0:T(8,128)(2,1)S(1)}, u32[]{:S(2)}, u32[]{:S(2)}) collective-permute-start(bf16[128,512]{1,0:T(8,128)(2,1)S(1)} %maximum_select_fusion.1), channel_id=1, source_target_pairs={{0,256},{8,264},{16,272},{24,280},{32,288},{40,296},{48,304},{56,3... | collective-permute-start | bytes 393224 | tf_op jit(solution)/shard_map/ppermute | solution.py:287
  54.5 3.9 %collective-permute-start.22 = (bf16[128,512]{1,0:T(8,128)(2,1)S(1)}, bf16[128,512]{1,0:T(8,128)(2,1)S(1)}, u32[]{:S(2)}, u32[]{:S(2)}) collective-permute-start(bf16[128,512]{1,0:T(8,128)(2,1)S(1)} %maximum_select_fusion.1), channel_id=1, source_target_pairs={{0,384},{8,392},{16,400},{24,408},{32,416},{40,424},{48,432},{56,4... | collective-permute-start | bytes 393224 | tf_op jit(solution)/shard_map/ppermute | solution.py:287
  58.5 6.0 %collective-permute-start = (bf16[256,512]{1,0:T(8,128)(2,1)}, bf16[256,512]{1,0:T(8,128)(2,1)S(1)}, u32[]{:S(2)}, u32[]{:S(2)}) collective-permute-start(bf16[256,512]{1,0:T(8,128)(2,1)} %q_own.9), channel_id=1, source_target_pairs={{0,8},{8,0},{16,24},{24,16},{32,40},{40,32},{48,56},{56,48},{64,72... | collective-permute-start | bytes 786440 | tf_op jit(solution)/shard_map/ppermute | solution.py:268
  64.6 5.0 %collective-permute-done.22 = bf16[128,512]{1,0:T(8,128)(2,1)S(1)} collective-permute-done((bf16[128,512]{1,0:T(8,128)(2,1)S(1)}, bf16[128,512]{1,0:T(8,128)(2,1)S(1)}, u32[]{:S(2)}, u32[]{:S(2)}) %collective-permute-start.22) | collective-permute-done | bytes 131104 | tf_op jit(solution)/shard_map/ppermute | solution.py:287
  69.7 1.9 %collective-permute-start.23 = (bf16[4,128,512]{2,1,0:T(8,128)(2,1)S(1)}, bf16[4,128,512]{2,1,0:T(8,128)(2,1)S(1)}, u32[]{:S(2)}, u32[]{:S(2)}) collective-permute-start(bf16[4,128,512]{2,1,0:T(8,128)(2,1)S(1)} %pad_maximum_fusion.refs_0_), channel_id=1, source_target_pairs={{0,16},{8,120},{16,32},{24,8},{32,48},{40,24},{48,64},{56,40},{64,... | collective-permute-start | bytes 1572872 | tf_op jit(solution)/shard_map/ppermute | solution.py:290
  71.6 1.9 %collective-permute-start.4 = (bf16[512,512]{1,0:T(8,128)(2,1)}, bf16[512,512]{1,0:T(8,128)(2,1)}, u32[]{:S(2)}, u32[]{:S(2)}) collective-permute-start(bf16[512,512]{1,0:T(8,128)(2,1)} %collective-permute-done.3.refs_0_), channel_id=1, source_target_pairs={{0,16},{16,32},{24,8},{32,48},{40,24},{48,64},{56,40},{64,80},{72,... | collective-permute-start | bytes 1572872 | tf_op jit(solution)/shard_map/ppermute | solution.py:270
  73.6 3.8 %collective-permute-start.9 = (bf16[512,512]{1,0:T(8,128)(2,1)}, bf16[512,512]{1,0:T(8,128)(2,1)}, u32[]{:S(2)}, u32[]{:S(2)}) collective-permute-start(bf16[512,512]{1,0:T(8,128)(2,1)} %collective-permute-done.8.refs_1_), channel_id=1, source_target_pairs={{0,16},{16,32},{24,8},{32,48},{40,24},{48,64},{56,40},{64,80},{72,... | collective-permute-start | bytes 1572872 | tf_op jit(solution)/shard_map/ppermute | solution.py:271
  77.8 0.9 copy-done
  78.8 2.2 %attend.5 = (f32[544,256]{1,0:T(8,128)S(1)}, f32[544,256]{1,0:T(8,128)S(1)}) custom-call(s32[32]{0:T(128)S(1)} %concatenate.39.scal, s32[8,256]{1,0:T(8,128)S(1)} %concatenate.40.bounds, bf16[256,512]{1,0:T(8,128)(2,1)S(1)} %copy-done, bf16[256,512]{1,0:T(8,128)(2,1)S(1)} %collective-permute-done.q_par, bf16[512,512]{1,0:T(8,128)(2,1)S(1)} %pack.1.refs_0_), custom_call_target="tpu_custom_call" | custom-call | flops 268435456 | bytes 1048576 | tf_op jit(solution)/shard_map/attend/pallas_call | solution.py:123
  81.0 2.9 %collective-permute-start.24 = (bf16[4,128,512]{2,1,0:T(8,128)(2,1)S(1)}, bf16[4,128,512]{2,1,0:T(8,128)(2,1)S(1)}, u32[]{:S(2)}, u32[]{:S(2)}) collective-permute-start(bf16[4,128,512]{2,1,0:T(8,128)(2,1)S(1)} %collective-permute-done.23.refs_1_), channel_id=1, source_target_pairs={{0,16},{8,120},{16,32},{24,8},{32,48},{40,24},{48,64},{56,40},{64,... | collective-permute-start | bytes 1572872 | tf_op jit(solution)/shard_map/ppermute | solution.py:290
  83.9 3.9 %attend.6 = (f32[544,256]{1,0:T(8,128)S(1)}, f32[544,256]{1,0:T(8,128)S(1)}) custom-call(s32[32]{0:T(128)S(1)} %concatenate.39.scal, s32[8,256]{1,0:T(8,128)S(1)} %concatenate.40.bounds, bf16[256,512]{1,0:T(8,128)(2,1)S(1)} %copy-done, bf16[256,512]{1,0:T(8,128)(2,1)S(1)} %collective-permute-done.q_par, ...), custom_call_target="tpu_custom_call", output_to_operand_aliasing={{0}: (6, {}), {1}: (7, {})} | custom-call | flops 536870912 | bytes 1048576 | tf_op jit(solution)/shard_map/attend/pallas_call | solution.py:123
  87.8 4.4 %attend.7 = (f32[544,256]{1,0:T(8,128)S(1)}, f32[544,256]{1,0:T(8,128)S(1)}) custom-call(s32[32]{0:T(128)S(1)} %concatenate.39.scal, s32[8,256]{1,0:T(8,128)S(1)} %concatenate.40.bounds, bf16[256,512]{1,0:T(8,128)(2,1)S(1)} %copy-done, bf16[256,512]{1,0:T(8,128)(2,1)S(1)} %collective-permute-done.q_par, ...), custom_call_target="tpu_custom_call", output_to_operand_aliasing={{0}: (6, {}), {1}: (7, {})} | custom-call | flops 536870912 | bytes 1048576 | tf_op jit(solution)/shard_map/attend/pallas_call | solution.py:123
  92.2 4.6 %attend.8 = (f32[544,256]{1,0:T(8,128)S(1)}, f32[544,256]{1,0:T(8,128)S(1)}) custom-call(s32[32]{0:T(128)S(1)} %concatenate.39.scal, s32[8,256]{1,0:T(8,128)S(1)} %concatenate.40.bounds, bf16[256,512]{1,0:T(8,128)(2,1)S(1)} %copy-done, bf16[256,512]{1,0:T(8,128)(2,1)S(1)} %collective-permute-done.q_par, ...), custom_call_target="tpu_custom_call", output_to_operand_aliasing={{0}: (6, {}), {1}: (7, {})} | custom-call | flops 536870912 | bytes 1048576 | tf_op jit(solution)/shard_map/attend/pallas_call | solution.py:123
  96.8 3.1 %attend.9 = (f32[544,256]{1,0:T(8,128)S(1)}, f32[544,256]{1,0:T(8,128)S(1)}) custom-call(s32[32]{0:T(128)S(1)} %concatenate.39.scal, s32[8,256]{1,0:T(8,128)S(1)} %concatenate.40.bounds, bf16[256,512]{1,0:T(8,128)(2,1)S(1)} %copy-done, bf16[256,512]{1,0:T(8,128)(2,1)S(1)} %collective-permute-done.q_par, ...), custom_call_target="tpu_custom_call", output_to_operand_aliasing={{0}: (6, {}), {1}: (7, {})} | custom-call | flops 536870912 | bytes 1048576 | tf_op jit(solution)/shard_map/attend/pallas_call | solution.py:123
  99.9 1.9 %collective-permute-start.10 = (f32[544,256]{1,0:T(8,128)S(1)}, f32[544,256]{1,0:T(8,128)S(1)}, u32[]{:S(2)}, u32[]{:S(2)}) collective-permute-start(f32[544,256]{1,0:T(8,128)S(1)} %get-tuple-element.24), channel_id=1, source_target_pairs={{0,8},{8,0},{16,24},{24,16},{32,40},{40,32},{48,56},{56,48},{64,72... | collective-permute-start | bytes 1671176 | tf_op jit(solution)/shard_map/ppermute | solution.py:294
  101.9 1.9 %collective-permute-start.25 = (bf16[4,128,512]{2,1,0:T(8,128)(2,1)S(1)}, bf16[4,128,512]{2,1,0:T(8,128)(2,1)S(1)}, u32[]{:S(2)}, u32[]{:S(2)}) collective-permute-start(bf16[4,128,512]{2,1,0:T(8,128)(2,1)S(1)} %collective-permute-done.24.refs_2_), channel_id=1, source_target_pairs={{0,16},{8,120},{16,32},{24,8},{32,48},{40,24},{48,64},{56,40},{64,... | collective-permute-start | bytes 1572872 | tf_op jit(solution)/shard_map/ppermute | solution.py:290
  103.8 2.4 %collective-permute-start.27 = (bf16[4,128,512]{2,1,0:T(8,128)(2,1)S(1)}, bf16[4,128,512]{2,1,0:T(8,128)(2,1)S(1)}, u32[]{:S(2)}, u32[]{:S(2)}) collective-permute-start(bf16[4,128,512]{2,1,0:T(8,128)(2,1)S(1)} %collective-permute-done.23.refs_1_), channel_id=1, source_target_pairs={{0,8},{8,0},{16,24},{24,16},{32,40},{40,32},{48,56},{56,48},{64,72... | collective-permute-start | bytes 1572872 | tf_op jit(solution)/shard_map/ppermute | solution.py:291
  106.4 7.4 %collective-permute-start.11 = (bf16[256,512]{1,0:T(8,128)(2,1)S(1)}, bf16[256,512]{1,0:T(8,128)(2,1)S(1)}, u32[]{:S(2)}, u32[]{:S(2)}) collective-permute-start(bf16[256,512]{1,0:T(8,128)(2,1)S(1)} %merge.1.refs_0_), channel_id=1, source_target_pairs={{0,1},{1,2},{2,3},{3,4},{4,5},{5,6},{6,7},{7,0},{8,9},{9,10},{10,1... | collective-permute-start | bytes 786440 | tf_op jit(solution)/shard_map/ppermute | solution.py:298
  113.8 4.5 %collective-permute-start.15 = (bf16[256,512]{1,0:T(8,128)(2,1)S(1)}, bf16[256,512]{1,0:T(8,128)(2,1)S(1)}, u32[]{:S(2)}, u32[]{:S(2)}) collective-permute-start(bf16[256,512]{1,0:T(8,128)(2,1)S(1)} %merge.1.refs_0_), channel_id=1, source_target_pairs={{0,7},{1,0},{2,1},{3,2},{4,3},{5,4},{6,5},{7,6},{8,15},{9,8},{10,9... | collective-permute-start | bytes 786440 | tf_op jit(solution)/shard_map/ppermute | solution.py:300
  118.3 4.5 %collective-permute-done.11.refs_1_ = bf16[256,512]{1,0:T(8,128)(2,1)S(1)} collective-permute-done((bf16[256,512]{1,0:T(8,128)(2,1)S(1)}, bf16[256,512]{1,0:T(8,128)(2,1)S(1)}, u32[]{:S(2)}, u32[]{:S(2)}) %collective-permute-start.11) | collective-permute-done | bytes 262176 | tf_op jit(solution)/shard_map/ppermute | solution.py:298
  122.9 1.9 %collective-permute-start.12 = (bf16[256,512]{1,0:T(8,128)(2,1)S(1)}, bf16[256,512]{1,0:T(8,128)(2,1)S(1)}, u32[]{:S(2)}, u32[]{:S(2)}) collective-permute-start(bf16[256,512]{1,0:T(8,128)(2,1)S(1)} %collective-permute-done.11.refs_1_), channel_id=1, source_target_pairs={{0,1},{1,2},{2,3},{3,4},{4,5},{5,6},{6,7},{7,0},{8,9},{9,10},{10,1... | collective-permute-start | bytes 786440 | tf_op jit(solution)/shard_map/ppermute | solution.py:298
  124.8 1.9 %collective-permute-start.28 = (bf16[4,128,512]{2,1,0:T(8,128)(2,1)S(1)}, bf16[4,128,512]{2,1,0:T(8,128)(2,1)S(1)}, u32[]{:S(2)}, u32[]{:S(2)}) collective-permute-start(bf16[4,128,512]{2,1,0:T(8,128)(2,1)S(1)} %collective-permute-done.24.refs_2_), channel_id=1, source_target_pairs={{0,8},{8,0},{16,24},{24,16},{32,40},{40,32},{48,56},{56,48},{64,72... | collective-permute-start | bytes 1572872 | tf_op jit(solution)/shard_map/ppermute | solution.py:291
  126.7 4.9 %collective-permute-start.26 = (bf16[4,128,512]{2,1,0:T(8,128)(2,1)S(1)}, bf16[4,128,512]{2,1,0:T(8,128)(2,1)S(1)}, u32[]{:S(2)}, u32[]{:S(2)}) collective-permute-start(bf16[4,128,512]{2,1,0:T(8,128)(2,1)S(1)} %collective-permute-done.25.refs_3_), channel_id=1, source_target_pairs={{0,16},{8,120},{16,32},{24,8},{32,48},{40,24},{48,64},{56,40},{64,... | collective-permute-start | bytes 1572872 | tf_op jit(solution)/shard_map/ppermute | solution.py:290
  131.6 1.9 %collective-permute-start.29 = (bf16[4,128,512]{2,1,0:T(8,128)(2,1)S(1)}, bf16[4,128,512]{2,1,0:T(8,128)(2,1)S(1)}, u32[]{:S(2)}, u32[]{:S(2)}) collective-permute-start(bf16[4,128,512]{2,1,0:T(8,128)(2,1)S(1)} %collective-permute-done.25.refs_3_), channel_id=1, source_target_pairs={{0,8},{8,0},{16,24},{24,16},{32,40},{40,32},{48,56},{56,48},{64,72... | collective-permute-start | bytes 1572872 | tf_op jit(solution)/shard_map/ppermute | solution.py:291
  133.5 5.1 %collective-permute-start.16 = (bf16[256,512]{1,0:T(8,128)(2,1)S(1)}, bf16[256,512]{1,0:T(8,128)(2,1)S(1)}, u32[]{:S(2)}, u32[]{:S(2)}) collective-permute-start(bf16[256,512]{1,0:T(8,128)(2,1)S(1)} %collective-permute-done.15.refs_4_), channel_id=1, source_target_pairs={{0,7},{1,0},{2,1},{3,2},{4,3},{5,4},{6,5},{7,6},{8,15},{9,8},{10,9... | collective-permute-start | bytes 786440 | tf_op jit(solution)/shard_map/ppermute | solution.py:300
  138.7 1.9 %collective-permute-start.13 = (bf16[256,512]{1,0:T(8,128)(2,1)S(1)}, bf16[256,512]{1,0:T(8,128)(2,1)S(1)}, u32[]{:S(2)}, u32[]{:S(2)}) collective-permute-start(bf16[256,512]{1,0:T(8,128)(2,1)S(1)} %collective-permute-done.12.refs_2_), channel_id=1, source_target_pairs={{0,1},{1,2},{2,3},{3,4},{4,5},{5,6},{6,7},{7,0},{8,9},{9,10},{10,1... | collective-permute-start | bytes 786440 | tf_op jit(solution)/shard_map/ppermute | solution.py:298
  140.6 4.3 %collective-permute-done.16.refs_5_ = bf16[256,512]{1,0:T(8,128)(2,1)S(1)} collective-permute-done((bf16[256,512]{1,0:T(8,128)(2,1)S(1)}, bf16[256,512]{1,0:T(8,128)(2,1)S(1)}, u32[]{:S(2)}, u32[]{:S(2)}) %collective-permute-start.16) | collective-permute-done | bytes 262176 | tf_op jit(solution)/shard_map/ppermute | solution.py:300
  144.9 5.6 %collective-permute-start.17 = (bf16[256,512]{1,0:T(8,128)(2,1)S(1)}, bf16[256,512]{1,0:T(8,128)(2,1)S(1)}, u32[]{:S(2)}, u32[]{:S(2)}) collective-permute-start(bf16[256,512]{1,0:T(8,128)(2,1)S(1)} %collective-permute-done.16.refs_5_), channel_id=1, source_target_pairs={{0,7},{1,0},{2,1},{3,2},{4,3},{5,4},{6,5},{7,6},{8,15},{9,8},{10,9... | collective-permute-start | bytes 786440 | tf_op jit(solution)/shard_map/ppermute | solution.py:300
  150.5 1.9 %collective-permute-start.14 = (bf16[256,512]{1,0:T(8,128)(2,1)S(1)}, bf16[256,512]{1,0:T(8,128)(2,1)S(1)}, u32[]{:S(2)}, u32[]{:S(2)}) collective-permute-start(bf16[256,512]{1,0:T(8,128)(2,1)S(1)} %collective-permute-done.13.refs_3_), channel_id=1, source_target_pairs={{0,1},{1,2},{2,3},{3,4},{4,5},{5,6},{6,7},{7,0},{8,9},{9,10},{10,1... | collective-permute-start | bytes 786440 | tf_op jit(solution)/shard_map/ppermute | solution.py:298
  153.3 1.0 project.2.refs_3_
  154.4 1.5 collective-permute-done.17.refs_1_
  155.8 5.3 %collective-permute-done.14.refs_0_ = bf16[256,512]{1,0:T(8,128)(2,1)S(1)} collective-permute-done((bf16[256,512]{1,0:T(8,128)(2,1)S(1)}, bf16[256,512]{1,0:T(8,128)(2,1)S(1)}, u32[]{:S(2)}, u32[]{:S(2)}) %collective-permute-start.14) | collective-permute-done | bytes 262176 | tf_op jit(solution)/shard_map/ppermute | solution.py:298
  161.2 1.2 project.3
  (45 shorter events, 2.9 us)
Async XLA Ops:
  0.0 0.9 copy-start.1
  1.0 0.9 copy-start.2
  2.0 4.2 %collective-permute-start.5 = (bf16[512,512]{1,0:T(8,128)(2,1)S(1)}, bf16[512,512]{1,0:T(8,128)(2,1)S(1)}, u32[]{:S(2)}, u32[]{:S(2)}) collective-permute-start(bf16[512,512]{1,0:T(8,128)(2,1)S(1)} %pack.1.refs_0_), channel_id=1, source_target_pairs={{0,8},{8,0},{16,24},{24,16},{32,40},{40,32},{48,56},{56,48},{64,72... | collective-permute-start | bytes 1572872 | tf_op jit(solution)/shard_map/ppermute | solution.py:267
  3.9 11.1 %collective-permute-start.1 = (bf16[512,512]{1,0:T(8,128)(2,1)S(1)}, bf16[512,512]{1,0:T(8,128)(2,1)S(1)}, u32[]{:S(2)}, u32[]{:S(2)}) collective-permute-start(bf16[512,512]{1,0:T(8,128)(2,1)S(1)} %pack.1.refs_0_), channel_id=1, source_target_pairs={{0,16},{16,32},{24,8},{32,48},{40,24},{48,64},{56,40},{64,80},{72,... | collective-permute-start | bytes 1572872 | tf_op jit(solution)/shard_map/ppermute | solution.py:270
  6.2 14.4 %collective-permute-start.6 = (bf16[512,512]{1,0:T(8,128)(2,1)S(1)}, bf16[512,512]{1,0:T(8,128)(2,1)S(1)}, u32[]{:S(2)}, u32[]{:S(2)}) collective-permute-start(bf16[512,512]{1,0:T(8,128)(2,1)S(1)} %collective-permute-done.5), channel_id=1, source_target_pairs={{0,16},{16,32},{24,8},{32,48},{40,24},{48,64},{56,40},{64,80},{72,... | collective-permute-start | bytes 1572872 | tf_op jit(solution)/shard_map/ppermute | solution.py:271
  15.0 30.7 %collective-permute-start.2 = (bf16[512,512]{1,0:T(8,128)(2,1)S(1)}, bf16[512,512]{1,0:T(8,128)(2,1)S(1)}, u32[]{:S(2)}, u32[]{:S(2)}) collective-permute-start(bf16[512,512]{1,0:T(8,128)(2,1)S(1)} %collective-permute-done.1.refs_0_), channel_id=1, source_target_pairs={{0,16},{16,32},{24,8},{32,48},{40,24},{48,64},{56,40},{64,80},{72,... | collective-permute-start | bytes 1572872 | tf_op jit(solution)/shard_map/ppermute | solution.py:270
  20.6 27.1 %collective-permute-start.7 = (bf16[512,512]{1,0:T(8,128)(2,1)S(1)}, bf16[512,512]{1,0:T(8,128)(2,1)}, u32[]{:S(2)}, u32[]{:S(2)}) collective-permute-start(bf16[512,512]{1,0:T(8,128)(2,1)S(1)} %collective-permute-done.6.refs_1_), channel_id=1, source_target_pairs={{0,16},{16,32},{24,8},{32,48},{40,24},{48,64},{56,40},{64,80},{72,... | collective-permute-start | bytes 1572872 | tf_op jit(solution)/shard_map/ppermute | solution.py:271
  25.0 18.8 %collective-permute-start.18 = (bf16[64,512]{1,0:T(8,128)(2,1)}, bf16[64,512]{1,0:T(8,128)(2,1)S(1)}, u32[]{:S(2)}, u32[]{:S(2)}) collective-permute-start(bf16[64,512]{1,0:T(8,128)(2,1)} %bitcast.27), channel_id=1, source_target_pairs={{0,0},{8,8},{16,16},{24,24},{32,32},{40,40},{48,48},{56,56},{1,64}... | collective-permute-start | bytes 196616 | tf_op jit(solution)/shard_map/ppermute | solution.py:278
  43.8 6.8 %collective-permute-start.19 = (bf16[64,512]{1,0:T(8,128)(2,1)S(1)}, bf16[64,512]{1,0:T(8,128)(2,1)S(1)}, u32[]{:S(2)}, u32[]{:S(2)}) collective-permute-start(bf16[64,512]{1,0:T(8,128)(2,1)S(1)} %collective-permute-done.18), channel_id=1, source_target_pairs={{0,8},{8,0},{16,24},{24,16},{32,40},{40,32},{48,56},{56,48},{64,72... | collective-permute-start | bytes 196616 | tf_op jit(solution)/shard_map/ppermute | solution.py:279
  45.7 25.9 %collective-permute-start.3 = (bf16[512,512]{1,0:T(8,128)(2,1)S(1)}, bf16[512,512]{1,0:T(8,128)(2,1)}, u32[]{:S(2)}, u32[]{:S(2)}) collective-permute-start(bf16[512,512]{1,0:T(8,128)(2,1)S(1)} %collective-permute-done.2.refs_0_), channel_id=1, source_target_pairs={{0,16},{16,32},{24,8},{32,48},{40,24},{48,64},{56,40},{64,80},{72,... | collective-permute-start | bytes 1572872 | tf_op jit(solution)/shard_map/ppermute | solution.py:270
  47.7 25.9 %collective-permute-start.8 = (bf16[512,512]{1,0:T(8,128)(2,1)}, bf16[512,512]{1,0:T(8,128)(2,1)}, u32[]{:S(2)}, u32[]{:S(2)}) collective-permute-start(bf16[512,512]{1,0:T(8,128)(2,1)} %collective-permute-done.7.refs_1_), channel_id=1, source_target_pairs={{0,16},{16,32},{24,8},{32,48},{40,24},{48,64},{56,40},{64,80},{72,... | collective-permute-start | bytes 1572872 | tf_op jit(solution)/shard_map/ppermute | solution.py:271
  50.6 7.9 %collective-permute-start.20 = (bf16[128,512]{1,0:T(8,128)(2,1)S(1)}, bf16[128,512]{1,0:T(8,128)(2,1)S(1)}, u32[]{:S(2)}, u32[]{:S(2)}) collective-permute-start(bf16[128,512]{1,0:T(8,128)(2,1)S(1)} %maximum_select_fusion.1), channel_id=1, source_target_pairs={{0,128},{8,136},{16,144},{24,152},{32,160},{40,168},{48,176},{56,1... | collective-permute-start | bytes 393224 | tf_op jit(solution)/shard_map/ppermute | solution.py:287
  52.5 12.0 %collective-permute-start.21 = (bf16[128,512]{1,0:T(8,128)(2,1)S(1)}, bf16[128,512]{1,0:T(8,128)(2,1)S(1)}, u32[]{:S(2)}, u32[]{:S(2)}) collective-permute-start(bf16[128,512]{1,0:T(8,128)(2,1)S(1)} %maximum_select_fusion.1), channel_id=1, source_target_pairs={{0,256},{8,264},{16,272},{24,280},{32,288},{40,296},{48,304},{56,3... | collective-permute-start | bytes 393224 | tf_op jit(solution)/shard_map/ppermute | solution.py:287
  54.5 15.2 %collective-permute-start.22 = (bf16[128,512]{1,0:T(8,128)(2,1)S(1)}, bf16[128,512]{1,0:T(8,128)(2,1)S(1)}, u32[]{:S(2)}, u32[]{:S(2)}) collective-permute-start(bf16[128,512]{1,0:T(8,128)(2,1)S(1)} %maximum_select_fusion.1), channel_id=1, source_target_pairs={{0,384},{8,392},{16,400},{24,408},{32,416},{40,424},{48,432},{56,4... | collective-permute-start | bytes 393224 | tf_op jit(solution)/shard_map/ppermute | solution.py:287
  58.5 19.3 %collective-permute-start = (bf16[256,512]{1,0:T(8,128)(2,1)}, bf16[256,512]{1,0:T(8,128)(2,1)S(1)}, u32[]{:S(2)}, u32[]{:S(2)}) collective-permute-start(bf16[256,512]{1,0:T(8,128)(2,1)} %q_own.9), channel_id=1, source_target_pairs={{0,8},{8,0},{16,24},{24,16},{32,40},{40,32},{48,56},{56,48},{64,72... | collective-permute-start | bytes 786440 | tf_op jit(solution)/shard_map/ppermute | solution.py:268
  69.7 11.3 %collective-permute-start.23 = (bf16[4,128,512]{2,1,0:T(8,128)(2,1)S(1)}, bf16[4,128,512]{2,1,0:T(8,128)(2,1)S(1)}, u32[]{:S(2)}, u32[]{:S(2)}) collective-permute-start(bf16[4,128,512]{2,1,0:T(8,128)(2,1)S(1)} %pad_maximum_fusion.refs_0_), channel_id=1, source_target_pairs={{0,16},{8,120},{16,32},{24,8},{32,48},{40,24},{48,64},{56,40},{64,... | collective-permute-start | bytes 1572872 | tf_op jit(solution)/shard_map/ppermute | solution.py:290
  71.6 25.1 %collective-permute-start.4 = (bf16[512,512]{1,0:T(8,128)(2,1)}, bf16[512,512]{1,0:T(8,128)(2,1)}, u32[]{:S(2)}, u32[]{:S(2)}) collective-permute-start(bf16[512,512]{1,0:T(8,128)(2,1)} %collective-permute-done.3.refs_0_), channel_id=1, source_target_pairs={{0,16},{16,32},{24,8},{32,48},{40,24},{48,64},{56,40},{64,80},{72,... | collective-permute-start | bytes 1572872 | tf_op jit(solution)/shard_map/ppermute | solution.py:270
  73.6 23.2 %collective-permute-start.9 = (bf16[512,512]{1,0:T(8,128)(2,1)}, bf16[512,512]{1,0:T(8,128)(2,1)}, u32[]{:S(2)}, u32[]{:S(2)}) collective-permute-start(bf16[512,512]{1,0:T(8,128)(2,1)} %collective-permute-done.8.refs_1_), channel_id=1, source_target_pairs={{0,16},{16,32},{24,8},{32,48},{40,24},{48,64},{56,40},{64,80},{72,... | collective-permute-start | bytes 1572872 | tf_op jit(solution)/shard_map/ppermute | solution.py:271
  77.8 1.0 copy-start
  81.0 20.9 %collective-permute-start.24 = (bf16[4,128,512]{2,1,0:T(8,128)(2,1)S(1)}, bf16[4,128,512]{2,1,0:T(8,128)(2,1)S(1)}, u32[]{:S(2)}, u32[]{:S(2)}) collective-permute-start(bf16[4,128,512]{2,1,0:T(8,128)(2,1)S(1)} %collective-permute-done.23.refs_1_), channel_id=1, source_target_pairs={{0,16},{8,120},{16,32},{24,8},{32,48},{40,24},{48,64},{56,40},{64,... | collective-permute-start | bytes 1572872 | tf_op jit(solution)/shard_map/ppermute | solution.py:290
  99.9 6.3 %collective-permute-start.10 = (f32[544,256]{1,0:T(8,128)S(1)}, f32[544,256]{1,0:T(8,128)S(1)}, u32[]{:S(2)}, u32[]{:S(2)}) collective-permute-start(f32[544,256]{1,0:T(8,128)S(1)} %get-tuple-element.24), channel_id=1, source_target_pairs={{0,8},{8,0},{16,24},{24,16},{32,40},{40,32},{48,56},{56,48},{64,72... | collective-permute-start | bytes 1671176 | tf_op jit(solution)/shard_map/ppermute | solution.py:294
  101.9 24.8 %collective-permute-start.25 = (bf16[4,128,512]{2,1,0:T(8,128)(2,1)S(1)}, bf16[4,128,512]{2,1,0:T(8,128)(2,1)S(1)}, u32[]{:S(2)}, u32[]{:S(2)}) collective-permute-start(bf16[4,128,512]{2,1,0:T(8,128)(2,1)S(1)} %collective-permute-done.24.refs_2_), channel_id=1, source_target_pairs={{0,16},{8,120},{16,32},{24,8},{32,48},{40,24},{48,64},{56,40},{64,... | collective-permute-start | bytes 1572872 | tf_op jit(solution)/shard_map/ppermute | solution.py:290
  103.8 27.8 %collective-permute-start.27 = (bf16[4,128,512]{2,1,0:T(8,128)(2,1)S(1)}, bf16[4,128,512]{2,1,0:T(8,128)(2,1)S(1)}, u32[]{:S(2)}, u32[]{:S(2)}) collective-permute-start(bf16[4,128,512]{2,1,0:T(8,128)(2,1)S(1)} %collective-permute-done.23.refs_1_), channel_id=1, source_target_pairs={{0,8},{8,0},{16,24},{24,16},{32,40},{40,32},{48,56},{56,48},{64,72... | collective-permute-start | bytes 1572872 | tf_op jit(solution)/shard_map/ppermute | solution.py:291
  106.4 16.4 %collective-permute-start.11 = (bf16[256,512]{1,0:T(8,128)(2,1)S(1)}, bf16[256,512]{1,0:T(8,128)(2,1)S(1)}, u32[]{:S(2)}, u32[]{:S(2)}) collective-permute-start(bf16[256,512]{1,0:T(8,128)(2,1)S(1)} %merge.1.refs_0_), channel_id=1, source_target_pairs={{0,1},{1,2},{2,3},{3,4},{4,5},{5,6},{6,7},{7,0},{8,9},{9,10},{10,1... | collective-permute-start | bytes 786440 | tf_op jit(solution)/shard_map/ppermute | solution.py:298
  113.8 19.7 %collective-permute-start.15 = (bf16[256,512]{1,0:T(8,128)(2,1)S(1)}, bf16[256,512]{1,0:T(8,128)(2,1)S(1)}, u32[]{:S(2)}, u32[]{:S(2)}) collective-permute-start(bf16[256,512]{1,0:T(8,128)(2,1)S(1)} %merge.1.refs_0_), channel_id=1, source_target_pairs={{0,7},{1,0},{2,1},{3,2},{4,3},{5,4},{6,5},{7,6},{8,15},{9,8},{10,9... | collective-permute-start | bytes 786440 | tf_op jit(solution)/shard_map/ppermute | solution.py:300
  122.9 15.8 %collective-permute-start.12 = (bf16[256,512]{1,0:T(8,128)(2,1)S(1)}, bf16[256,512]{1,0:T(8,128)(2,1)S(1)}, u32[]{:S(2)}, u32[]{:S(2)}) collective-permute-start(bf16[256,512]{1,0:T(8,128)(2,1)S(1)} %collective-permute-done.11.refs_1_), channel_id=1, source_target_pairs={{0,1},{1,2},{2,3},{3,4},{4,5},{5,6},{6,7},{7,0},{8,9},{9,10},{10,1... | collective-permute-start | bytes 786440 | tf_op jit(solution)/shard_map/ppermute | solution.py:298
  124.8 27.6 %collective-permute-start.28 = (bf16[4,128,512]{2,1,0:T(8,128)(2,1)S(1)}, bf16[4,128,512]{2,1,0:T(8,128)(2,1)S(1)}, u32[]{:S(2)}, u32[]{:S(2)}) collective-permute-start(bf16[4,128,512]{2,1,0:T(8,128)(2,1)S(1)} %collective-permute-done.24.refs_2_), channel_id=1, source_target_pairs={{0,8},{8,0},{16,24},{24,16},{32,40},{40,32},{48,56},{56,48},{64,72... | collective-permute-start | bytes 1572872 | tf_op jit(solution)/shard_map/ppermute | solution.py:291
  126.7 25.7 %collective-permute-start.26 = (bf16[4,128,512]{2,1,0:T(8,128)(2,1)S(1)}, bf16[4,128,512]{2,1,0:T(8,128)(2,1)S(1)}, u32[]{:S(2)}, u32[]{:S(2)}) collective-permute-start(bf16[4,128,512]{2,1,0:T(8,128)(2,1)S(1)} %collective-permute-done.25.refs_3_), channel_id=1, source_target_pairs={{0,16},{8,120},{16,32},{24,8},{32,48},{40,24},{48,64},{56,40},{64,... | collective-permute-start | bytes 1572872 | tf_op jit(solution)/shard_map/ppermute | solution.py:290
  131.6 20.8 %collective-permute-start.29 = (bf16[4,128,512]{2,1,0:T(8,128)(2,1)S(1)}, bf16[4,128,512]{2,1,0:T(8,128)(2,1)S(1)}, u32[]{:S(2)}, u32[]{:S(2)}) collective-permute-start(bf16[4,128,512]{2,1,0:T(8,128)(2,1)S(1)} %collective-permute-done.25.refs_3_), channel_id=1, source_target_pairs={{0,8},{8,0},{16,24},{24,16},{32,40},{40,32},{48,56},{56,48},{64,72... | collective-permute-start | bytes 1572872 | tf_op jit(solution)/shard_map/ppermute | solution.py:291
  133.5 11.3 %collective-permute-start.16 = (bf16[256,512]{1,0:T(8,128)(2,1)S(1)}, bf16[256,512]{1,0:T(8,128)(2,1)S(1)}, u32[]{:S(2)}, u32[]{:S(2)}) collective-permute-start(bf16[256,512]{1,0:T(8,128)(2,1)S(1)} %collective-permute-done.15.refs_4_), channel_id=1, source_target_pairs={{0,7},{1,0},{2,1},{3,2},{4,3},{5,4},{6,5},{7,6},{8,15},{9,8},{10,9... | collective-permute-start | bytes 786440 | tf_op jit(solution)/shard_map/ppermute | solution.py:300
  138.7 11.8 %collective-permute-start.13 = (bf16[256,512]{1,0:T(8,128)(2,1)S(1)}, bf16[256,512]{1,0:T(8,128)(2,1)S(1)}, u32[]{:S(2)}, u32[]{:S(2)}) collective-permute-start(bf16[256,512]{1,0:T(8,128)(2,1)S(1)} %collective-permute-done.12.refs_2_), channel_id=1, source_target_pairs={{0,1},{1,2},{2,3},{3,4},{4,5},{5,6},{6,7},{7,0},{8,9},{9,10},{10,1... | collective-permute-start | bytes 786440 | tf_op jit(solution)/shard_map/ppermute | solution.py:298
  144.9 10.9 %collective-permute-start.17 = (bf16[256,512]{1,0:T(8,128)(2,1)S(1)}, bf16[256,512]{1,0:T(8,128)(2,1)S(1)}, u32[]{:S(2)}, u32[]{:S(2)}) collective-permute-start(bf16[256,512]{1,0:T(8,128)(2,1)S(1)} %collective-permute-done.16.refs_5_), channel_id=1, source_target_pairs={{0,7},{1,0},{2,1},{3,2},{4,3},{5,4},{6,5},{7,6},{8,15},{9,8},{10,9... | collective-permute-start | bytes 786440 | tf_op jit(solution)/shard_map/ppermute | solution.py:300
  150.5 10.7 %collective-permute-start.14 = (bf16[256,512]{1,0:T(8,128)(2,1)S(1)}, bf16[256,512]{1,0:T(8,128)(2,1)S(1)}, u32[]{:S(2)}, u32[]{:S(2)}) collective-permute-start(bf16[256,512]{1,0:T(8,128)(2,1)S(1)} %collective-permute-done.13.refs_3_), channel_id=1, source_target_pairs={{0,1},{1,2},{2,3},{3,4},{4,5},{5,6},{6,7},{7,0},{8,9},{9,10},{10,1... | collective-permute-start | bytes 786440 | tf_op jit(solution)/shard_map/ppermute | solution.py:298
